TPU v7x, 32 devices: a whole 2x2x4 slice. The times are simulated.
32 devices in a mesh: band: 2 (over x), stn: 8 (over z, y), tile: 2 (over core).
Axes of the slice: x: 2, y: 2, z: 4, core: 2. Of those that a mesh axis runs over, the one named last changes fastest.
Arguments:
- raw_samples: float32 [2, 4096, 8240], P(None, ('band', 'stn', 'tile')), parts along dimension 1, may hold values from -6 to 6
- prototype: float32 [64], replicated, may hold values from -0.75 to 0.75
- beam_weight: bfloat16 [2, 512, 4096], P(None, None, ('band', 'stn', 'tile')), parts along dimension 2, may hold values from -0.09375 to 0.09375
Outputs:
- visibility: bfloat16 [64, 2, 2048, 2048], P(('band', 'stn'), None, None, 'tile'), parts along dimension 0
- beam_out: float32 [2, 64, 512, 256], P(None, ('band', 'stn'), 'tile'), parts along dimension 1
There are 2 independent parts, one for each index of `band`. A program takes and returns all parts, laid end to end along the dimension named above; an argument that names none is the same for every part. Nothing has to cross between parts.
All inputs are finite; a program needn't handle non-finite values.
Results may differ from a plain program's by a relative error of at most 0.0055.
Values may be sent and summed in bfloat16 or wider, within the bound.
A program may use at most 192 MiB of HBM per device.

v0:
```python
import functools
import math

import jax
import jax.numpy as jnp
from jax import lax
from jax.experimental import pallas as pl
from jax.experimental.pallas import tpu as pltpu
from jax.sharding import PartitionSpec as P


FINE = 16
TAPS = 4
NBEAM = 512
DUMPS = 2
MD = 256


def filter_table(prototype):
    taps_fine = prototype.shape[0]
    sample = jnp.arange(taps_fine, dtype=jnp.int32) % FINE
    channel = jnp.arange(FINE, dtype=jnp.int32)
    phase_index = sample[:, None] * channel[None, :] % FINE
    phase_angle = phase_index.astype(jnp.float32) * (2.0 * math.pi / FINE)
    return (prototype[:, None] * jnp.cos(phase_angle), -prototype[:, None] * jnp.sin(phase_angle))


def channelize(raw_samples, prototype):
    table_re, table_im = filter_table(prototype)
    inputs_here = raw_samples.shape[1]
    frames = DUMPS * MD
    shaped = raw_samples.reshape(2, inputs_here, frames + TAPS - 1, FINE).transpose(0, 3, 1, 2)
    windows = jnp.concatenate(
        [shaped[:, :, :, offset : offset + frames] for offset in range(TAPS)], axis=1
    )
    highest = lax.Precision.HIGHEST
    spec_re = jnp.einsum("nk,nbm->kbm", table_re, windows[0], precision=highest) - jnp.einsum(
        "nk,nbm->kbm", table_im, windows[1], precision=highest
    )
    spec_im = jnp.einsum("nk,nbm->kbm", table_im, windows[0], precision=highest) + jnp.einsum(
        "nk,nbm->kbm", table_re, windows[1], precision=highest
    )
    spectra = jnp.stack([spec_re, spec_im]).astype(jnp.bfloat16)
    spectra = spectra.reshape(2, FINE, inputs_here, DUMPS, MD).transpose(0, 1, 3, 2, 4)
    return spectra.reshape(2, FINE * DUMPS, inputs_here, MD)


def form_beams(weights, rows_data):
    real_rows = jnp.concatenate([weights[0], -weights[1]], axis=1)
    imag_rows = jnp.concatenate([weights[1], weights[0]], axis=1)
    stacked = jnp.concatenate([rows_data[0], rows_data[1]], axis=1)
    beam_re = jnp.einsum("bn,snm->sbm", real_rows, stacked, preferred_element_type=jnp.float32)
    beam_im = jnp.einsum("bn,snm->sbm", imag_rows, stacked, preferred_element_type=jnp.float32)
    return jnp.stack([beam_re, beam_im])


def to_listed(weight_all, stations, cores, per_block):
    beams_here = weight_all.shape[1]
    weight_listed = weight_all.reshape(2, beams_here, stations, cores, per_block).transpose(
        0, 1, 3, 2, 4
    )
    return weight_listed.reshape(2, beams_here, stations * cores * per_block)


def per_device_plain(raw_samples, prototype, beam_weight):
    spectra = channelize(raw_samples, prototype)
    turned = lax.all_to_all(spectra, "stn", split_axis=1, concat_axis=2, tiled=True)
    col_left = jnp.concatenate([turned[0], turned[1]], axis=2)
    col_twist = jnp.concatenate([-turned[1], turned[0]], axis=2)
    beam_half = NBEAM // lax.axis_size("tile")
    stations = lax.axis_size("stn")
    cores = lax.axis_size("tile")
    per_block = beam_weight.shape[2]
    all_rows = lax.all_gather(turned, "tile", axis=2, tiled=True)
    row_left = jnp.concatenate([all_rows[0], all_rows[1]], axis=2)
    vis_re = jnp.einsum("snf,shf->snh", row_left, col_left, preferred_element_type=jnp.float32)
    vis_im = jnp.einsum("snf,shf->snh", row_left, col_twist, preferred_element_type=jnp.float32)
    visibility = (jnp.stack([vis_re, vis_im], axis=1) * (1.0 / MD)).astype(jnp.bfloat16)
    weight_all = lax.all_gather(beam_weight, ("stn", "tile"), axis=2, tiled=True)
    weight_listed = to_listed(weight_all, stations, cores, per_block)
    weight_mine = lax.dynamic_slice_in_dim(
        weight_listed, lax.axis_index("tile") * beam_half, beam_half, 1
    )
    beam_out = form_beams(weight_mine, all_rows)
    return (visibility, beam_out)


GROUP = 8
LANES = 128
STEP = 1024
SPAN = GROUP * FINE + (TAPS - 1) * FINE
TAIL = (TAPS - 1) * FINE


def window_table(prototype, channel):
    taps_fine = prototype.shape[0]
    sample = jnp.arange(taps_fine, dtype=jnp.int32) % FINE
    phase_index = channel[:, None] * sample[None, :] % FINE
    phase_angle = phase_index.astype(jnp.float32) * (2.0 * math.pi / FINE)
    re = prototype[None, :] * jnp.cos(phase_angle)
    im = -prototype[None, :] * jnp.sin(phase_angle)
    both = jnp.stack([jnp.stack([re, -im], axis=1), jnp.stack([im, re], axis=1)], axis=1)
    shifted = jnp.stack(
        [
            jnp.pad(both, ((0, 0), (0, 0), (0, 0), (FINE * f, SPAN - taps_fine - FINE * f)))
            for f in range(GROUP)
        ],
        axis=2,
    )
    table = shifted.reshape(channel.shape[0] * 2 * GROUP, 2 * SPAN)
    high = lax.reduce_precision(table, 8, 7)
    low = (table - high).astype(jnp.bfloat16)
    high = high.astype(jnp.bfloat16)
    return jnp.concatenate([high, low, high], axis=1)


def channelize_kernel(tokens, table_ref, main_ref, next_ref, *refs):
    outs, window = refs[tokens:-1], refs[-1]
    groups = STEP // (GROUP * FINE)
    for part in range(2):
        samples = jnp.concatenate([main_ref[part], next_ref[part, :TAIL]], axis=0)
        high = samples.astype(jnp.bfloat16)
        low = (samples - high.astype(jnp.float32)).astype(jnp.bfloat16)
        for j in range(groups):
            rows = slice(j * GROUP * FINE, j * GROUP * FINE + SPAN)
            cols = slice(j * LANES, (j + 1) * LANES)
            window[part * SPAN : (part + 1) * SPAN, cols] = high[rows]
            window[(2 + part) * SPAN : (3 + part) * SPAN, cols] = high[rows]
            window[(4 + part) * SPAN : (5 + part) * SPAN, cols] = low[rows]
    done = jnp.dot(table_ref[...], window[...], preferred_element_type=jnp.float32)
    lead = outs[0].shape[0]
    for n in range(len(outs) * lead):
        for part in range(2):
            row = (n * 2 + part) * GROUP
            for j in range(0, groups, 2):
                pair = jnp.concatenate(
                    [
                        done[row : row + GROUP, j * LANES : (j + 1) * LANES],
                        done[row : row + GROUP, (j + 1) * LANES : (j + 2) * LANES],
                    ],
                    axis=0,
                )
                at = slice(j * GROUP, (j + 2) * GROUP)
                outs[n // lead][n % lead, part, at, :] = pair.astype(jnp.bfloat16)


def channelize_dump(turned, table, dump, count, lead, after):
    inputs_here = turned.shape[2]
    steps = MD * FINE // STEP
    frames = STEP // FINE
    ahead = 64
    out = jax.ShapeDtypeStruct((lead, 2, MD, inputs_here), jnp.bfloat16)
    return pl.pallas_call(
        functools.partial(channelize_kernel, len(after)),
        grid=(steps,),
        in_specs=[
            pl.BlockSpec(table.shape, lambda i: (0, 0)),
            pl.BlockSpec((2, STEP, inputs_here), lambda i: (0, dump * steps + i, 0)),
            pl.BlockSpec(
                (2, ahead, inputs_here),
                lambda i: (0, (dump * steps + i + 1) * (STEP // ahead), 0),
            ),
        ]
        + [pl.BlockSpec(memory_space=pl.ANY)] * len(after),
        out_specs=[pl.BlockSpec((lead, 2, frames, inputs_here), lambda i: (0, 0, i, 0))] * count,
        out_shape=[out] * count,
        scratch_shapes=[
            pltpu.VMEM((table.shape[1], STEP // (GROUP * FINE) * LANES), jnp.bfloat16)
        ],
        compiler_params=pltpu.CompilerParams(vmem_limit_bytes=58 << 20),
        cost_estimate=pl.CostEstimate(
            flops=2 * table.shape[0] * table.shape[1] * steps * 1024,
            bytes_accessed=inputs_here * MD * FINE * 12,
            transcendentals=0,
        ),
    )(table, turned, turned, *after)


def place_kernel(count, where_ref, *refs):
    ins, out = refs[:count], refs[-1]
    r = 0
    for ref in ins:
        pieces, _, two, rows, _ = ref.shape
        for n in range(pieces):
            at = pl.ds(pl.multiple_of(where_ref[r] * LANES, LANES), LANES)
            for b in range(two):
                out[0, b * rows : (b + 1) * rows, at] = ref[n, 0, b]
            r += 1


def place(blocks, where, after):
    lead, two, rows, width = blocks[0].shape[1:]
    total = width * sum(block.shape[0] for block in blocks)
    return pl.pallas_call(
        functools.partial(place_kernel, len(blocks)),
        grid_spec=pltpu.PrefetchScalarGridSpec(
            num_scalar_prefetch=1,
            grid=(lead,),
            in_specs=[
                pl.BlockSpec((block.shape[0], 1, two, rows, width), lambda i, w: (0, i, 0, 0, 0))
                for block in blocks
            ]
            + [pl.BlockSpec(memory_space=pl.ANY)] * len(after),
            out_specs=pl.BlockSpec((1, two * rows, total), lambda i, w: (i, 0, 0)),
        ),
        out_shape=jax.ShapeDtypeStruct((lead, two * rows, total), blocks[0].dtype),
        compiler_params=pltpu.CompilerParams(vmem_limit_bytes=30 << 20),
        cost_estimate=pl.CostEstimate(
            flops=0, bytes_accessed=4 * lead * two * rows * total, transcendentals=0
        ),
    )(where, *blocks, *after)


def correlate_kernel(rows, tile_ref, left_ref, right_ref, *refs):
    out_ref, twist = refs[-2], refs[-1]
    step = pl.program_id(1)

    @pl.when(step == 0)
    def _():
        twist[:MD] = -right_ref[0, MD:]
        twist[MD:] = right_ref[0, :MD]

    left = left_ref[0, :, pl.ds(pl.multiple_of(step * rows, rows), rows)].T
    re = jnp.dot(left, right_ref[0], preferred_element_type=jnp.float32)
    out_ref[0, 0] = (re * (1.0 / MD)).astype(jnp.bfloat16)
    im = jnp.dot(left, twist[...], preferred_element_type=jnp.float32)
    out_ref[0, 1] = (im * (1.0 / MD)).astype(jnp.bfloat16)


def correlate(left, right, half, slots, first, before):
    kh, depth, width = right.shape
    rows = 512
    steps = width // rows
    spec = pl.BlockSpec((1, depth, width), lambda k, a, t: (k, 0, 0))
    held = [] if before is None else [before]
    return pl.pallas_call(
        functools.partial(correlate_kernel, rows),
        grid_spec=pltpu.PrefetchScalarGridSpec(
            num_scalar_prefetch=1,
            grid=(kh, steps),
            in_specs=[spec, spec] + [pl.BlockSpec(memory_space=pl.ANY)] * len(held),
            out_specs=pl.BlockSpec(
                (1, 2, rows, width),
                lambda k, a, t: (k * DUMPS + first, 0, a + t[0] * steps, 0),
            ),
            scratch_shapes=[pltpu.VMEM((depth, width), jnp.bfloat16)],
        ),
        out_shape=jax.ShapeDtypeStruct((slots, 2, 2 * width, width), jnp.bfloat16),
        input_output_aliases={3: 0} if held else {},
        compiler_params=pltpu.CompilerParams(vmem_limit_bytes=40 << 20),
        cost_estimate=pl.CostEstimate(
            flops=kh * 2 * 2 * width * width * depth,
            bytes_accessed=kh * 2 * 2 * width * width,
            transcendentals=0,
        ),
    )(half, left, right, *held)


def beam_kernel(own_w, other_w, own_ref, other_ref, *refs):
    out_ref = refs[-1]
    dims = (((1,), (1,)), ((), ()))
    both = lax.dot_general(own_w[0], own_ref[0], dims, preferred_element_type=jnp.float32)
    both += lax.dot_general(other_w[0], other_ref[0], dims, preferred_element_type=jnp.float32)
    beams = own_w.shape[1] // 2
    out_ref[0, 0] = both[:beams, :MD] - both[beams:, MD:]
    out_ref[1, 0] = both[beams:, :MD] + both[:beams, MD:]


def beams_of(weights, own, other, slots, first, before):
    kh, depth, width = own.shape
    rows = weights.shape[1]
    held = [] if before is None else [before]
    moving = pl.BlockSpec((1, depth, width), lambda k: (k, 0, 0))
    return pl.pallas_call(
        beam_kernel,
        grid=(kh,),
        in_specs=[
            pl.BlockSpec((1, rows, width), lambda k: (0, 0, 0)),
            pl.BlockSpec((1, rows, width), lambda k: (1, 0, 0)),
            moving,
            moving,
        ]
        + [pl.BlockSpec(memory_space=pl.ANY)] * len(held),
        out_specs=pl.BlockSpec((2, 1, rows // 2, MD), lambda k: (0, k * DUMPS + first, 0, 0)),
        out_shape=jax.ShapeDtypeStruct((2, slots, rows // 2, MD), jnp.float32),
        input_output_aliases={4: 0} if held else {},
        compiler_params=pltpu.CompilerParams(vmem_limit_bytes=40 << 20),
        cost_estimate=pl.CostEstimate(
            flops=kh * 4 * rows * width * depth,
            bytes_accessed=kh * 4 * width * depth + 4 * rows * width,
            transcendentals=0,
        ),
    )(weights, weights, own, other, *held)


def partners(count, mask):
    return [(a, a ^ mask) for a in range(count)]


def per_device_fast(raw_samples, prototype, beam_weight):
    stations = lax.axis_size("stn")
    me, tile = lax.axis_index("stn"), lax.axis_index("tile")
    slots = FINE * DUMPS // stations
    kh = slots // DUMPS
    where = me ^ jnp.arange(stations, dtype=jnp.int32)
    channel = (where[:, None] * kh + jnp.arange(kh, dtype=jnp.int32)[None, :]).reshape(-1)
    table = window_table(prototype, channel)
    beam_half = beam_weight.shape[1] // 2
    swap = [(0, 1), (1, 0)]

    mine = lax.dynamic_slice_in_dim(beam_weight, tile * beam_half, beam_half, 1)
    theirs = lax.dynamic_slice_in_dim(beam_weight, (1 - tile) * beam_half, beam_half, 1)
    held = [jnp.stack([mine, lax.ppermute(theirs, "tile", swap)])[None]]
    order, stages, mask = [0], [], stations // 2
    while mask:
        whole = jnp.concatenate(held) if len(held) > 1 else held[0]
        held = [whole, lax.ppermute(whole, "stn", partners(stations, mask))]
        order = order + [o ^ mask for o in order]
        stages.append(held[1])
        mask //= 2

    turned = raw_samples.transpose(0, 2, 1)
    parts = []
    for dump in range(DUMPS):
        after = [parts[-1][0], stages[0]] if parts else []
        lead = 1 if dump else kh
        count = stations * kh // lead
        parts.append(channelize_dump(turned, table, dump, count, lead, after))

    chunks = [(0, list(range(kh)))] + [(d, [k]) for d in range(1, DUMPS) for k in range(kh)]
    arrived = []
    for dump, ks in chunks:
        blocks = [None] * stations
        for r in reversed(range(stations)):
            sent = parts[dump][r if dump == 0 else r * kh + ks[0]][None]
            blocks[r] = lax.ppermute(sent, "stn", partners(stations, r)) if r else sent
        arrived.append(blocks)

    visibility, beam_out, weights, after = None, None, None, [stages[1 % len(stages)], parts[-1][0]]
    own_half = tile.reshape(1).astype(jnp.int32)
    for n, (dump, ks) in enumerate(chunks):
        first = ks[0] * DUMPS + dump
        own = place(arrived[n], where, after)
        other = lax.ppermute(own, "tile", swap)
        visibility = correlate(own, own, own_half, slots, first, visibility)
        visibility = correlate(other, own, 1 - own_half, slots, first, visibility)
        if weights is None:
            spots = me ^ jnp.asarray(order, dtype=jnp.int32)
            weights = place(held, spots, [])
        beam_out = beams_of(weights, own, other, slots, first, beam_out)
        after = [visibility, beam_out] if n else [visibility]
    return visibility, beam_out


def per_device(raw_samples, prototype, beam_weight):
    stations = lax.axis_size("stn")
    fits = (
        raw_samples.shape[1] == LANES
        and lax.axis_size("tile") == 2
        and stations & (stations - 1) == 0
        and FINE % stations == 0
    )
    if fits:
        return per_device_fast(raw_samples, prototype, beam_weight)
    return per_device_plain(raw_samples, prototype, beam_weight)


def solution(mesh):
    placed = (P(None, ("band", "stn", "tile"), None), P(), P(None, None, ("band", "stn", "tile")))
    return jax.shard_map(
        per_device,
        mesh=mesh,
        in_specs=placed,
        out_specs=(P(("band", "stn"), None, None, "tile"), P(None, ("band", "stn"), "tile", None)),
        check_vma=False,
    )
```

profile of v0, /device:TPU:9, one launch (start us, length us, event | category | flops | bytes accessed | tf_op | source)
XLA Modules:
  0.0 169.1 jit_solution(5789109730539080823)
XLA Ops:
  5.5 2.4 %collective-permute-start.1 = (bf16[1,2,2,256,128]{4,3,2,1,0:T(8,128)(2,1)S(1)}, bf16[1,2,2,256,128]{4,3,2,1,0:T(8,128)(2,1)S(1)}, u32[]{:S(2)}, u32[]{:S(2)}) collective-permute-start(bf16[1,2,2,256,128]{4,3,2,1,0:T(8,128)(2,1)S(1)} %maximum_bitcast_fusion), channel_id=1, source_target_pairs={{0,8},{2,10},{4,12},{6,14},{8,0},{10,2},{12,4},{14,6},{1,9},{3,11}... | collective-permute-start | bytes 786440 | tf_op jit(solution)/shard_map/ppermute | solution.py:317
  9.1 6.7 %shard_map.59 = (bf16[2,2,256,128]{3,2,1,0:T(8,128)(2,1)}, bf16[2,2,256,128]{3,2,1,0:T(8,128)(2,1)}, bf16[2,2,256,128]{3,2,1,0:T(8,128)(2,1)}, bf16[2,2,256,128]...) custom-call(bf16[256,1056]{1,0:T(8,128)(2,1)} %concatenate.10.table_, ...), custom_call_target="tpu_custom_call" | custom-call | flops 2214592512 | bytes 6291456 | tf_op jit(solution)/shard_map/pallas_call | solution.py:153
  20.5 2.4 %collective-permute-start.19 = (bf16[1,2,2,256,128]{4,3,2,1,0:T(8,128)(2,1)}, bf16[1,2,2,256,128]{4,3,2,1,0:T(8,128)(2,1)S(1)}, u32[]{:S(2)}, u32[]{:S(2)}) collective-permute-start(bf16[1,2,2,256,128]{4,3,2,1,0:T(8,128)(2,1)} %bitcast.62), channel_id=1, source_target_pairs={{0,8},{2,10},{4,12},{6,14},{8,0},{10,2},{12,4},{14,6},{1,9},{3,11}... | collective-permute-start | bytes 786440 | tf_op jit(solution)/shard_map/ppermute | solution.py:336
  24.7 12.9 %collective-permute-start.21 = (bf16[1,2,2,256,128]{4,3,2,1,0:T(8,128)(2,1)}, bf16[1,2,2,256,128]{4,3,2,1,0:T(8,128)(2,1)S(1)}, u32[]{:S(2)}, u32[]{:S(2)}) collective-permute-start(bf16[1,2,2,256,128]{4,3,2,1,0:T(8,128)(2,1)} %bitcast.60), channel_id=1, source_target_pairs={{0,12},{2,14},{4,8},{6,10},{8,4},{10,6},{12,0},{14,2},{1,13},{3,15... | collective-permute-start | bytes 786440 | tf_op jit(solution)/shard_map/ppermute | solution.py:336
  37.6 2.6 %collective-permute-done.18.refs_3_ = bf16[1,2,2,256,128]{4,3,2,1,0:T(8,128)(2,1)S(1)} collective-permute-done((bf16[1,2,2,256,128]{4,3,2,1,0:T(8,128)(2,1)}, bf16[1,2,2,256,128]{4,3,2,1,0:T(8,128)(2,1)S(1)}, u32[]{:S(2)}, u32[]{:S(2)}) %collective-permute-start.18) | collective-permute-done | bytes 262176 | tf_op jit(solution)/shard_map/ppermute | solution.py:336
  40.2 4.0 %collective-permute-start.22 = (bf16[1,2,2,256,128]{4,3,2,1,0:T(8,128)(2,1)}, bf16[1,2,2,256,128]{4,3,2,1,0:T(8,128)(2,1)S(1)}, u32[]{:S(2)}, u32[]{:S(2)}) collective-permute-start(bf16[1,2,2,256,128]{4,3,2,1,0:T(8,128)(2,1)} %bitcast.59), channel_id=1, source_target_pairs={{0,14},{2,12},{4,10},{6,8},{8,6},{10,4},{12,2},{14,0},{1,15},{3,13... | collective-permute-start | bytes 786440 | tf_op jit(solution)/shard_map/ppermute | solution.py:336
  44.2 6.9 %shard_map.60 = (bf16[1,2,256,128]{3,2,1,0:T(8,128)(2,1)}, bf16[1,2,256,128]{3,2,1,0:T(8,128)(2,1)}, bf16[1,2,256,128]{3,2,1,0:T(8,128)(2,1)}, bf16[1,2,256,128]...) custom-call(bf16[256,1056]{1,0:T(8,128)(2,1)} %concatenate.10.table_, ...), custom_call_target="tpu_custom_call" | custom-call | flops 2214592512 | bytes 6291456 | tf_op jit(solution)/shard_map/pallas_call | solution.py:153
  51.7 14.6 %collective-permute-done.21.refs_6_ = bf16[1,2,2,256,128]{4,3,2,1,0:T(8,128)(2,1)S(1)} collective-permute-done((bf16[1,2,2,256,128]{4,3,2,1,0:T(8,128)(2,1)}, bf16[1,2,2,256,128]{4,3,2,1,0:T(8,128)(2,1)S(1)}, u32[]{:S(2)}, u32[]{:S(2)}) %collective-permute-start.21) | collective-permute-done | bytes 262176 | tf_op jit(solution)/shard_map/ppermute | solution.py:336
  66.3 6.8 %collective-permute-done.22.refs_7_ = bf16[1,2,2,256,128]{4,3,2,1,0:T(8,128)(2,1)S(1)} collective-permute-done((bf16[1,2,2,256,128]{4,3,2,1,0:T(8,128)(2,1)}, bf16[1,2,2,256,128]{4,3,2,1,0:T(8,128)(2,1)S(1)}, u32[]{:S(2)}, u32[]{:S(2)}) %collective-permute-start.22) | collective-permute-done | bytes 262176 | tf_op jit(solution)/shard_map/ppermute | solution.py:336
  78.9 2.1 %collective-permute-start.13 = (bf16[1,1,2,256,128]{4,3,2,1,0:T(8,128)(2,1)}, bf16[1,1,2,256,128]{4,3,2,1,0:T(8,128)(2,1)S(1)}, u32[]{:S(2)}, u32[]{:S(2)}) collective-permute-start(bf16[1,1,2,256,128]{4,3,2,1,0:T(8,128)(2,1)} %bitcast.76), channel_id=1, source_target_pairs={{0,10},{2,8},{4,14},{6,12},{8,2},{10,0},{12,6},{14,4},{1,11},{3,9}... | collective-permute-start | bytes 393224 | tf_op jit(solution)/shard_map/ppermute | solution.py:336
  81.1 6.7 %shard_map.62.refs_0_ = bf16[4,2,2048,1024]{3,2,1,0:T(8,128)(2,1)} custom-call(s32[1]{0:T(128)} %bitcast.tile_ref, bf16[2,512,1024]{2,1,0:T(8,128)(2,1)S(1)} %shard_map.61.left_ref.right_ref.own_ref, bf16[2,512,1024]{2,1,0:T(8,128)(2,1)S(1)} %shard_map.61.left_ref.right_ref.own_ref), custom_call_target="tpu_custom_call" | custom-call | flops 4294967296 | bytes 8388608 | tf_op jit(solution)/shard_map/pallas_call | solution.py:236
  87.9 1.5 collective-permute-start.14
  91.0 6.7 %shard_map.63.refs_8_.refs_0_ = bf16[4,2,2048,1024]{3,2,1,0:T(8,128)(2,1)} custom-call(s32[1]{0:T(128)S(6)} %sub.11.tile_ref, bf16[2,512,1024]{2,1,0:T(8,128)(2,1)S(1)} %collective-permute-done.24.left_ref.other_ref, bf16[2,512,1024]{2,1,0:T(8,128)(2,1)S(1)} %shard_map.61.left_ref.right_ref.own_ref, ...), custom_call_target="tpu_custom_call", output_to_operand_aliasing={{}: (3, {})} | custom-call | flops 4294967296 | bytes 8388608 | tf_op jit(solution)/shard_map/pallas_call | solution.py:236
  97.7 2.4 %collective-permute-done.14.refs_6_ = bf16[1,1,2,256,128]{4,3,2,1,0:T(8,128)(2,1)S(1)} collective-permute-done((bf16[1,1,2,256,128]{4,3,2,1,0:T(8,128)(2,1)S(1)}, bf16[1,1,2,256,128]{4,3,2,1,0:T(8,128)(2,1)S(1)}, u32[]{:S(2)}, u32[]{:S(2)}) %collective-permute-start.14) | collective-permute-done | bytes 131104 | tf_op jit(solution)/shard_map/ppermute | solution.py:336
  100.1 3.1 %collective-permute-done.15.refs_7_ = bf16[1,1,2,256,128]{4,3,2,1,0:T(8,128)(2,1)S(1)} collective-permute-done((bf16[1,1,2,256,128]{4,3,2,1,0:T(8,128)(2,1)S(1)}, bf16[1,1,2,256,128]{4,3,2,1,0:T(8,128)(2,1)S(1)}, u32[]{:S(2)}, u32[]{:S(2)}) %collective-permute-start.15) | collective-permute-done | bytes 131104 | tf_op jit(solution)/shard_map/ppermute | solution.py:336
  103.2 15.1 %collective-permute-done.9.refs_1_ = bf16[1,1,2,256,128]{4,3,2,1,0:T(8,128)(2,1)S(1)} collective-permute-done((bf16[1,1,2,256,128]{4,3,2,1,0:T(8,128)(2,1)S(1)}, bf16[1,1,2,256,128]{4,3,2,1,0:T(8,128)(2,1)S(1)}, u32[]{:S(2)}, u32[]{:S(2)}) %collective-permute-start.9) | collective-permute-done | bytes 131104 | tf_op jit(solution)/shard_map/ppermute | solution.py:336
  119.2 2.4 %collective-permute-start.25 = (bf16[1,512,1024]{2,1,0:T(8,128)(2,1)S(1)}, bf16[1,512,1024]{2,1,0:T(8,128)(2,1)S(1)}, u32[]{:S(2)}, u32[]{:S(2)}) collective-permute-start(bf16[1,512,1024]{2,1,0:T(8,128)(2,1)S(1)} %shard_map.64.left_ref.right_ref.own_ref), channel_id=1, source_target_pairs={{0,1},{1,0},{2,3},{3,2},{4,5},{5,4},{6,7},{7,6},{8,9},{9,8},{10,11... | collective-permute-start | bytes 3145736 | tf_op jit(solution)/shard_map/ppermute | solution.py:344
  122.4 1.5 collective-permute-start.3
  125.0 2.1 %collective-permute-start.5 = (bf16[1,1,2,256,128]{4,3,2,1,0:T(8,128)(2,1)S(1)}, bf16[1,1,2,256,128]{4,3,2,1,0:T(8,128)(2,1)S(1)}, u32[]{:S(2)}, u32[]{:S(2)}) collective-permute-start(bf16[1,1,2,256,128]{4,3,2,1,0:T(8,128)(2,1)S(1)} %bitcast.69), channel_id=1, source_target_pairs={{0,8},{2,10},{4,12},{6,14},{8,0},{10,2},{12,4},{14,6},{1,9},{3,11}... | collective-permute-start | bytes 393224 | tf_op jit(solution)/shard_map/ppermute | solution.py:336
  128.4 4.0 %shard_map.65.refs_0_ = bf16[4,2,2048,1024]{3,2,1,0:T(8,128)(2,1)} custom-call(s32[1]{0:T(128)} %bitcast.tile_ref, bf16[1,512,1024]{2,1,0:T(8,128)(2,1)S(1)} %shard_map.64.left_ref.right_ref.own_ref, bf16[1,512,1024]{2,1,0:T(8,128)(2,1)S(1)} %shard_map.64.left_ref.right_ref.own_ref, ...), custom_call_target="tpu_custom_call", output_to_operand_aliasing={{}: (3, {})} | custom-call | flops 2147483648 | bytes 4194304 | tf_op jit(solution)/shard_map/pallas_call | solution.py:236
  132.4 3.4 %shard_map.68.refs_0_ = f32[2,4,256,256]{3,2,1,0:T(8,128)} custom-call(bf16[2,512,1024]{2,1,0:T(8,128)(2,1)S(1)} %shard_map.67.own_w.other_w, bf16[2,512,1024]{2,1,0:T(8,128)(2,1)S(1)} %shard_map.67.own_w.other_w, bf16[2,512,1024]{2,1,0:T(8,128)(2,1)S(1)} %shard_map.61.left_ref.right_ref.own_ref, ...), custom_call_target="tpu_custom_call" | custom-call | flops 2147483648 | bytes 6291456 | tf_op jit(solution)/shard_map/pallas_call | solution.py:274
  137.1 1.4 collective-permute-start.8
  138.5 4.0 %shard_map.66.refs_8_.refs_0_ = bf16[4,2,2048,1024]{3,2,1,0:T(8,128)(2,1)} custom-call(s32[1]{0:T(128)S(6)} %sub.11.tile_ref, bf16[1,512,1024]{2,1,0:T(8,128)(2,1)S(1)} %collective-permute-done.25.left_ref.other_ref, bf16[1,512,1024]{2,1,0:T(8,128)(2,1)S(1)} %shard_map.64.left_ref.right_ref.own_ref, ...), custom_call_target="tpu_custom_call", output_to_operand_aliasing={{}: (3, {})} | custom-call | flops 2147483648 | bytes 4194304 | tf_op jit(solution)/shard_map/pallas_call | solution.py:236
  142.6 2.1 %shard_map.69.refs_9_.refs_0_ = f32[2,4,256,256]{3,2,1,0:T(8,128)} custom-call(bf16[2,512,1024]{2,1,0:T(8,128)(2,1)S(1)} %shard_map.67.own_w.other_w, bf16[2,512,1024]{2,1,0:T(8,128)(2,1)S(1)} %shard_map.67.own_w.other_w, bf16[1,512,1024]{2,1,0:T(8,128)(2,1)S(1)} %shard_map.64.left_ref.right_ref.own_ref, ...), custom_call_target="tpu_custom_call", output_to_operand_aliasing={{}: (4, {})} | custom-call | flops 1073741824 | bytes 4194304 | tf_op jit(solution)/shard_map/pallas_call | solution.py:274
  144.6 2.1 %collective-permute-done.6.refs_5_ = bf16[1,1,2,256,128]{4,3,2,1,0:T(8,128)(2,1)S(1)} collective-permute-done((bf16[1,1,2,256,128]{4,3,2,1,0:T(8,128)(2,1)S(1)}, bf16[1,1,2,256,128]{4,3,2,1,0:T(8,128)(2,1)S(1)}, u32[]{:S(2)}, u32[]{:S(2)}) %collective-permute-start.6) | collective-permute-done | bytes 131104 | tf_op jit(solution)/shard_map/ppermute | solution.py:336
  146.8 4.4 %collective-permute-done.7.refs_6_ = bf16[1,1,2,256,128]{4,3,2,1,0:T(8,128)(2,1)S(1)} collective-permute-done((bf16[1,1,2,256,128]{4,3,2,1,0:T(8,128)(2,1)S(1)}, bf16[1,1,2,256,128]{4,3,2,1,0:T(8,128)(2,1)S(1)}, u32[]{:S(2)}, u32[]{:S(2)}) %collective-permute-start.7) | collective-permute-done | bytes 131104 | tf_op jit(solution)/shard_map/ppermute | solution.py:336
  151.2 3.7 %collective-permute-done.8.refs_7_ = bf16[1,1,2,256,128]{4,3,2,1,0:T(8,128)(2,1)S(1)} collective-permute-done((bf16[1,1,2,256,128]{4,3,2,1,0:T(8,128)(2,1)S(1)}, bf16[1,1,2,256,128]{4,3,2,1,0:T(8,128)(2,1)S(1)}, u32[]{:S(2)}, u32[]{:S(2)}) %collective-permute-start.8) | collective-permute-done | bytes 131104 | tf_op jit(solution)/shard_map/ppermute | solution.py:336
  154.9 1.6 copy-done
  157.3 1.7 collective-permute-start.27
  159.0 4.0 %shard_map.71.refs_0_ = bf16[4,2,2048,1024]{3,2,1,0:T(8,128)(2,1)} custom-call(s32[1]{0:T(128)} %bitcast.tile_ref, bf16[1,512,1024]{2,1,0:T(8,128)(2,1)S(1)} %shard_map.70.left_ref.right_ref.own_ref, bf16[1,512,1024]{2,1,0:T(8,128)(2,1)S(1)} %shard_map.70.left_ref.right_ref.own_ref, ...), custom_call_target="tpu_custom_call", output_to_operand_aliasing={{}: (3, {})} | custom-call | flops 2147483648 | bytes 4194304 | tf_op jit(solution)/shard_map/pallas_call | solution.py:236
  163.0 2.1 %shard_map.73 = f32[2,4,256,256]{3,2,1,0:T(8,128)} custom-call(bf16[2,512,1024]{2,1,0:T(8,128)(2,1)S(1)} %shard_map.67.own_w.other_w, bf16[2,512,1024]{2,1,0:T(8,128)(2,1)S(1)} %shard_map.67.own_w.other_w, bf16[1,512,1024]{2,1,0:T(8,128)(2,1)S(1)} %shard_map.70.left_ref.right_ref.own_ref, ...), custom_call_target="tpu_custom_call", output_to_operand_aliasing={{}: (4, {})} | custom-call | flops 1073741824 | bytes 4194304 | tf_op jit(solution)/shard_map/pallas_call | solution.py:274
  165.1 4.0 %shard_map.72 = bf16[4,2,2048,1024]{3,2,1,0:T(8,128)(2,1)} custom-call(s32[1]{0:T(128)S(6)} %sub.11.tile_ref, bf16[1,512,1024]{2,1,0:T(8,128)(2,1)S(1)} %collective-permute-done.27.left_ref.other_ref, bf16[1,512,1024]{2,1,0:T(8,128)(2,1)S(1)} %shard_map.70.left_ref.right_ref.own_ref, ...), custom_call_target="tpu_custom_call", output_to_operand_aliasing={{}: (3, {})} | custom-call | flops 2147483648 | bytes 4194304 | tf_op jit(solution)/shard_map/pallas_call | solution.py:236
  (101 shorter events, 27.0 us)
Async XLA Ops:
  1.6 3.9 %collective-permute-start = (bf16[2,256,128]{2,1,0:T(8,128)(2,1)S(1)}, bf16[2,256,128]{2,1,0:T(8,128)(2,1)S(1)}, u32[]{:S(2)}, u32[]{:S(2)}) collective-permute-start(bf16[2,256,128]{2,1,0:T(8,128)(2,1)S(1)} %get-tuple-element.53), channel_id=1, source_target_pairs={{0,1},{1,0},{2,3},{3,2},{4,5},{5,4},{6,7},{7,6},{8,9},{9,8},{10,11... | collective-permute-start | bytes 393224 | tf_op jit(solution)/shard_map/ppermute | solution.py:313
  5.5 14.0 %collective-permute-start.1 = (bf16[1,2,2,256,128]{4,3,2,1,0:T(8,128)(2,1)S(1)}, bf16[1,2,2,256,128]{4,3,2,1,0:T(8,128)(2,1)S(1)}, u32[]{:S(2)}, u32[]{:S(2)}) collective-permute-start(bf16[1,2,2,256,128]{4,3,2,1,0:T(8,128)(2,1)S(1)} %maximum_bitcast_fusion), channel_id=1, source_target_pairs={{0,8},{2,10},{4,12},{6,14},{8,0},{10,2},{12,4},{14,6},{1,9},{3,11}... | collective-permute-start | bytes 786440 | tf_op jit(solution)/shard_map/ppermute | solution.py:317
  15.9 7.8 %collective-permute-start.16 = (bf16[1,2,2,256,128]{4,3,2,1,0:T(8,128)(2,1)}, bf16[1,2,2,256,128]{4,3,2,1,0:T(8,128)(2,1)S(1)}, u32[]{:S(2)}, u32[]{:S(2)}) collective-permute-start(bf16[1,2,2,256,128]{4,3,2,1,0:T(8,128)(2,1)} %bitcast.65), channel_id=1, source_target_pairs={{0,2},{2,0},{4,6},{6,4},{8,10},{10,8},{12,14},{14,12},{1,3},{3,1},... | collective-permute-start | bytes 786440 | tf_op jit(solution)/shard_map/ppermute | solution.py:336
  17.2 7.5 %collective-permute-start.17 = (bf16[1,2,2,256,128]{4,3,2,1,0:T(8,128)(2,1)}, bf16[1,2,2,256,128]{4,3,2,1,0:T(8,128)(2,1)S(1)}, u32[]{:S(2)}, u32[]{:S(2)}) collective-permute-start(bf16[1,2,2,256,128]{4,3,2,1,0:T(8,128)(2,1)} %bitcast.64), channel_id=1, source_target_pairs={{0,4},{2,6},{4,0},{6,2},{8,12},{10,14},{12,8},{14,10},{1,5},{3,7},... | collective-permute-start | bytes 786440 | tf_op jit(solution)/shard_map/ppermute | solution.py:336
  17.3 22.9 %collective-permute-start.18 = (bf16[1,2,2,256,128]{4,3,2,1,0:T(8,128)(2,1)}, bf16[1,2,2,256,128]{4,3,2,1,0:T(8,128)(2,1)S(1)}, u32[]{:S(2)}, u32[]{:S(2)}) collective-permute-start(bf16[1,2,2,256,128]{4,3,2,1,0:T(8,128)(2,1)} %bitcast.63), channel_id=1, source_target_pairs={{0,6},{2,4},{4,2},{6,0},{8,14},{10,12},{12,10},{14,8},{1,7},{3,5},... | collective-permute-start | bytes 786440 | tf_op jit(solution)/shard_map/ppermute | solution.py:336
  19.5 24.6 %copy-start.5 = (bf16[1,2,2,256,128]{4,3,2,1,0:T(8,128)(2,1)}, bf16[1,2,2,256,128]{4,3,2,1,0:T(8,128)(2,1)S(1)}, u32[]{:S(2)}) copy-start(bf16[1,2,2,256,128]{4,3,2,1,0:T(8,128)(2,1)S(1)} %collective-permute-done.1.refs_1_) | copy-start | bytes 786436
  19.6 53.5 %collective-permute-start.23 = (bf16[2,2,2,256,128]{4,3,2,1,0:T(8,128)(2,1)S(1)}, bf16[2,2,2,256,128]{4,3,2,1,0:T(8,128)(2,1)S(1)}, u32[]{:S(2)}, u32[]{:S(2)}) collective-permute-start(bf16[2,2,2,256,128]{4,3,2,1,0:T(8,128)(2,1)S(1)} %pad_maximum_fusion.1), channel_id=1, source_target_pairs={{0,4},{2,6},{4,0},{6,2},{8,12},{10,14},{12,8},{14,10},{1,5},{3,7},... | collective-permute-start | bytes 1572872 | tf_op jit(solution)/shard_map/ppermute | solution.py:317
  20.5 30.6 %collective-permute-start.19 = (bf16[1,2,2,256,128]{4,3,2,1,0:T(8,128)(2,1)}, bf16[1,2,2,256,128]{4,3,2,1,0:T(8,128)(2,1)S(1)}, u32[]{:S(2)}, u32[]{:S(2)}) collective-permute-start(bf16[1,2,2,256,128]{4,3,2,1,0:T(8,128)(2,1)} %bitcast.62), channel_id=1, source_target_pairs={{0,8},{2,10},{4,12},{6,14},{8,0},{10,2},{12,4},{14,6},{1,9},{3,11}... | collective-permute-start | bytes 786440 | tf_op jit(solution)/shard_map/ppermute | solution.py:336
  23.7 28.0 %collective-permute-start.20 = (bf16[1,2,2,256,128]{4,3,2,1,0:T(8,128)(2,1)}, bf16[1,2,2,256,128]{4,3,2,1,0:T(8,128)(2,1)S(1)}, u32[]{:S(2)}, u32[]{:S(2)}) collective-permute-start(bf16[1,2,2,256,128]{4,3,2,1,0:T(8,128)(2,1)} %bitcast.61), channel_id=1, source_target_pairs={{0,10},{2,8},{4,14},{6,12},{8,2},{10,0},{12,6},{14,4},{1,11},{3,9}... | collective-permute-start | bytes 786440 | tf_op jit(solution)/shard_map/ppermute | solution.py:336
  24.7 41.6 %collective-permute-start.21 = (bf16[1,2,2,256,128]{4,3,2,1,0:T(8,128)(2,1)}, bf16[1,2,2,256,128]{4,3,2,1,0:T(8,128)(2,1)S(1)}, u32[]{:S(2)}, u32[]{:S(2)}) collective-permute-start(bf16[1,2,2,256,128]{4,3,2,1,0:T(8,128)(2,1)} %bitcast.60), channel_id=1, source_target_pairs={{0,12},{2,14},{4,8},{6,10},{8,4},{10,6},{12,0},{14,2},{1,13},{3,15... | collective-permute-start | bytes 786440 | tf_op jit(solution)/shard_map/ppermute | solution.py:336
  40.2 32.9 %collective-permute-start.22 = (bf16[1,2,2,256,128]{4,3,2,1,0:T(8,128)(2,1)}, bf16[1,2,2,256,128]{4,3,2,1,0:T(8,128)(2,1)S(1)}, u32[]{:S(2)}, u32[]{:S(2)}) collective-permute-start(bf16[1,2,2,256,128]{4,3,2,1,0:T(8,128)(2,1)} %bitcast.59), channel_id=1, source_target_pairs={{0,14},{2,12},{4,10},{6,8},{8,6},{10,4},{12,2},{14,0},{1,15},{3,13... | collective-permute-start | bytes 786440 | tf_op jit(solution)/shard_map/ppermute | solution.py:336
  44.2 28.9 %copy-start.1 = (bf16[2,2,256,128]{3,2,1,0:T(8,128)(2,1)S(1)}, bf16[2,2,256,128]{3,2,1,0:T(8,128)(2,1)}, u32[]{:S(2)}) copy-start(bf16[2,2,256,128]{3,2,1,0:T(8,128)(2,1)} %get-tuple-element.26.refs_0_) | copy-start | bytes 786436
  75.2 15.5 %collective-permute-start.24 = (bf16[2,512,1024]{2,1,0:T(8,128)(2,1)S(1)}, bf16[2,512,1024]{2,1,0:T(8,128)(2,1)S(1)}, u32[]{:S(2)}, u32[]{:S(2)}) collective-permute-start(bf16[2,512,1024]{2,1,0:T(8,128)(2,1)S(1)} %shard_map.61.left_ref.right_ref.own_ref), channel_id=1, source_target_pairs={{0,1},{1,0},{2,3},{3,2},{4,5},{5,4},{6,7},{7,6},{8,9},{9,8},{10,11... | collective-permute-start | bytes 6291464 | tf_op jit(solution)/shard_map/ppermute | solution.py:344
  76.3 11.6 %collective-permute-start.10 = (bf16[1,1,2,256,128]{4,3,2,1,0:T(8,128)(2,1)}, bf16[1,1,2,256,128]{4,3,2,1,0:T(8,128)(2,1)S(1)}, u32[]{:S(2)}, u32[]{:S(2)}) collective-permute-start(bf16[1,1,2,256,128]{4,3,2,1,0:T(8,128)(2,1)} %bitcast.79), channel_id=1, source_target_pairs={{0,4},{2,6},{4,0},{6,2},{8,12},{10,14},{12,8},{14,10},{1,5},{3,7},... | collective-permute-start | bytes 393224 | tf_op jit(solution)/shard_map/ppermute | solution.py:336
  76.3 13.2 %collective-permute-start.11 = (bf16[1,1,2,256,128]{4,3,2,1,0:T(8,128)(2,1)}, bf16[1,1,2,256,128]{4,3,2,1,0:T(8,128)(2,1)S(1)}, u32[]{:S(2)}, u32[]{:S(2)}) collective-permute-start(bf16[1,1,2,256,128]{4,3,2,1,0:T(8,128)(2,1)} %bitcast.78), channel_id=1, source_target_pairs={{0,6},{2,4},{4,2},{6,0},{8,14},{10,12},{12,10},{14,8},{1,7},{3,5},... | collective-permute-start | bytes 393224 | tf_op jit(solution)/shard_map/ppermute | solution.py:336
  77.7 12.0 %collective-permute-start.12 = (bf16[1,1,2,256,128]{4,3,2,1,0:T(8,128)(2,1)}, bf16[1,1,2,256,128]{4,3,2,1,0:T(8,128)(2,1)S(1)}, u32[]{:S(2)}, u32[]{:S(2)}) collective-permute-start(bf16[1,1,2,256,128]{4,3,2,1,0:T(8,128)(2,1)} %bitcast.77), channel_id=1, source_target_pairs={{0,8},{2,10},{4,12},{6,14},{8,0},{10,2},{12,4},{14,6},{1,9},{3,11}... | collective-permute-start | bytes 393224 | tf_op jit(solution)/shard_map/ppermute | solution.py:336
  78.9 18.8 %collective-permute-start.13 = (bf16[1,1,2,256,128]{4,3,2,1,0:T(8,128)(2,1)}, bf16[1,1,2,256,128]{4,3,2,1,0:T(8,128)(2,1)S(1)}, u32[]{:S(2)}, u32[]{:S(2)}) collective-permute-start(bf16[1,1,2,256,128]{4,3,2,1,0:T(8,128)(2,1)} %bitcast.76), channel_id=1, source_target_pairs={{0,10},{2,8},{4,14},{6,12},{8,2},{10,0},{12,6},{14,4},{1,11},{3,9}... | collective-permute-start | bytes 393224 | tf_op jit(solution)/shard_map/ppermute | solution.py:336
  87.9 12.2 %collective-permute-start.14 = (bf16[1,1,2,256,128]{4,3,2,1,0:T(8,128)(2,1)S(1)}, bf16[1,1,2,256,128]{4,3,2,1,0:T(8,128)(2,1)S(1)}, u32[]{:S(2)}, u32[]{:S(2)}) collective-permute-start(bf16[1,1,2,256,128]{4,3,2,1,0:T(8,128)(2,1)S(1)} %bitcast.75), channel_id=1, source_target_pairs={{0,12},{2,14},{4,8},{6,10},{8,4},{10,6},{12,0},{14,2},{1,13},{3,15... | collective-permute-start | bytes 393224 | tf_op jit(solution)/shard_map/ppermute | solution.py:336
  89.4 35.6 %collective-permute-start.26 = (bf16[4,2,2,256,128]{4,3,2,1,0:T(8,128)(2,1)S(1)}, bf16[4,2,2,256,128]{4,3,2,1,0:T(8,128)(2,1)S(1)}, u32[]{:S(2)}, u32[]{:S(2)}) collective-permute-start(bf16[4,2,2,256,128]{4,3,2,1,0:T(8,128)(2,1)S(1)} %pad_maximum_fusion.refs_0_), channel_id=1, source_target_pairs={{0,2},{2,0},{4,6},{6,4},{8,10},{10,8},{12,14},{14,12},{1,3},{3,1},... | collective-permute-start | bytes 3145736 | tf_op jit(solution)/shard_map/ppermute | solution.py:317
  89.7 13.5 %collective-permute-start.15 = (bf16[1,1,2,256,128]{4,3,2,1,0:T(8,128)(2,1)S(1)}, bf16[1,1,2,256,128]{4,3,2,1,0:T(8,128)(2,1)S(1)}, u32[]{:S(2)}, u32[]{:S(2)}) collective-permute-start(bf16[1,1,2,256,128]{4,3,2,1,0:T(8,128)(2,1)S(1)} %bitcast.74), channel_id=1, source_target_pairs={{0,14},{2,12},{4,10},{6,8},{8,6},{10,4},{12,2},{14,0},{1,15},{3,13... | collective-permute-start | bytes 393224 | tf_op jit(solution)/shard_map/ppermute | solution.py:336
  90.7 27.6 %copy-start.3 = (bf16[1,2,256,128]{3,2,1,0:T(8,128)(2,1)S(1)}, bf16[1,2,256,128]{3,2,1,0:T(8,128)(2,1)}, u32[]{:S(2)}) copy-start(bf16[1,2,256,128]{3,2,1,0:T(8,128)(2,1)} %get-tuple-element.35.refs_9_) | copy-start | bytes 393220
  90.7 27.6 %collective-permute-start.9 = (bf16[1,1,2,256,128]{4,3,2,1,0:T(8,128)(2,1)S(1)}, bf16[1,1,2,256,128]{4,3,2,1,0:T(8,128)(2,1)S(1)}, u32[]{:S(2)}, u32[]{:S(2)}) collective-permute-start(bf16[1,1,2,256,128]{4,3,2,1,0:T(8,128)(2,1)S(1)} %bitcast.73), channel_id=1, source_target_pairs={{0,2},{2,0},{4,6},{6,4},{8,10},{10,8},{12,14},{14,12},{1,3},{3,1},... | collective-permute-start | bytes 393224 | tf_op jit(solution)/shard_map/ppermute | solution.py:336
  119.2 17.9 %collective-permute-start.25 = (bf16[1,512,1024]{2,1,0:T(8,128)(2,1)S(1)}, bf16[1,512,1024]{2,1,0:T(8,128)(2,1)S(1)}, u32[]{:S(2)}, u32[]{:S(2)}) collective-permute-start(bf16[1,512,1024]{2,1,0:T(8,128)(2,1)S(1)} %shard_map.64.left_ref.right_ref.own_ref), channel_id=1, source_target_pairs={{0,1},{1,0},{2,3},{3,2},{4,5},{5,4},{6,7},{7,6},{8,9},{9,8},{10,11... | collective-permute-start | bytes 3145736 | tf_op jit(solution)/shard_map/ppermute | solution.py:344
  121.6 14.3 %collective-permute-start.2 = (bf16[1,1,2,256,128]{4,3,2,1,0:T(8,128)(2,1)S(1)}, bf16[1,1,2,256,128]{4,3,2,1,0:T(8,128)(2,1)S(1)}, u32[]{:S(2)}, u32[]{:S(2)}) collective-permute-start(bf16[1,1,2,256,128]{4,3,2,1,0:T(8,128)(2,1)S(1)} %bitcast.72), channel_id=1, source_target_pairs={{0,2},{2,0},{4,6},{6,4},{8,10},{10,8},{12,14},{14,12},{1,3},{3,1},... | collective-permute-start | bytes 393224 | tf_op jit(solution)/shard_map/ppermute | solution.py:336
  122.4 13.8 %collective-permute-start.3 = (bf16[1,1,2,256,128]{4,3,2,1,0:T(8,128)(2,1)S(1)}, bf16[1,1,2,256,128]{4,3,2,1,0:T(8,128)(2,1)S(1)}, u32[]{:S(2)}, u32[]{:S(2)}) collective-permute-start(bf16[1,1,2,256,128]{4,3,2,1,0:T(8,128)(2,1)S(1)} %bitcast.71), channel_id=1, source_target_pairs={{0,4},{2,6},{4,0},{6,2},{8,12},{10,14},{12,8},{14,10},{1,5},{3,7},... | collective-permute-start | bytes 393224 | tf_op jit(solution)/shard_map/ppermute | solution.py:336
  123.8 20.8 %collective-permute-start.4 = (bf16[1,1,2,256,128]{4,3,2,1,0:T(8,128)(2,1)S(1)}, bf16[1,1,2,256,128]{4,3,2,1,0:T(8,128)(2,1)S(1)}, u32[]{:S(2)}, u32[]{:S(2)}) collective-permute-start(bf16[1,1,2,256,128]{4,3,2,1,0:T(8,128)(2,1)S(1)} %bitcast.70), channel_id=1, source_target_pairs={{0,6},{2,4},{4,2},{6,0},{8,14},{10,12},{12,10},{14,8},{1,7},{3,5},... | collective-permute-start | bytes 393224 | tf_op jit(solution)/shard_map/ppermute | solution.py:336
  125.0 19.6 %collective-permute-start.5 = (bf16[1,1,2,256,128]{4,3,2,1,0:T(8,128)(2,1)S(1)}, bf16[1,1,2,256,128]{4,3,2,1,0:T(8,128)(2,1)S(1)}, u32[]{:S(2)}, u32[]{:S(2)}) collective-permute-start(bf16[1,1,2,256,128]{4,3,2,1,0:T(8,128)(2,1)S(1)} %bitcast.69), channel_id=1, source_target_pairs={{0,8},{2,10},{4,12},{6,14},{8,0},{10,2},{12,4},{14,6},{1,9},{3,11}... | collective-permute-start | bytes 393224 | tf_op jit(solution)/shard_map/ppermute | solution.py:336
  135.9 10.9 %collective-permute-start.6 = (bf16[1,1,2,256,128]{4,3,2,1,0:T(8,128)(2,1)S(1)}, bf16[1,1,2,256,128]{4,3,2,1,0:T(8,128)(2,1)S(1)}, u32[]{:S(2)}, u32[]{:S(2)}) collective-permute-start(bf16[1,1,2,256,128]{4,3,2,1,0:T(8,128)(2,1)S(1)} %bitcast.68), channel_id=1, source_target_pairs={{0,10},{2,8},{4,14},{6,12},{8,2},{10,0},{12,6},{14,4},{1,11},{3,9}... | collective-permute-start | bytes 393224 | tf_op jit(solution)/shard_map/ppermute | solution.py:336
  136.2 15.0 %collective-permute-start.7 = (bf16[1,1,2,256,128]{4,3,2,1,0:T(8,128)(2,1)S(1)}, bf16[1,1,2,256,128]{4,3,2,1,0:T(8,128)(2,1)S(1)}, u32[]{:S(2)}, u32[]{:S(2)}) collective-permute-start(bf16[1,1,2,256,128]{4,3,2,1,0:T(8,128)(2,1)S(1)} %bitcast.67), channel_id=1, source_target_pairs={{0,12},{2,14},{4,8},{6,10},{8,4},{10,6},{12,0},{14,2},{1,13},{3,15... | collective-permute-start | bytes 393224 | tf_op jit(solution)/shard_map/ppermute | solution.py:336
  137.1 17.8 %collective-permute-start.8 = (bf16[1,1,2,256,128]{4,3,2,1,0:T(8,128)(2,1)S(1)}, bf16[1,1,2,256,128]{4,3,2,1,0:T(8,128)(2,1)S(1)}, u32[]{:S(2)}, u32[]{:S(2)}) collective-permute-start(bf16[1,1,2,256,128]{4,3,2,1,0:T(8,128)(2,1)S(1)} %bitcast.66), channel_id=1, source_target_pairs={{0,14},{2,12},{4,10},{6,8},{8,6},{10,4},{12,2},{14,0},{1,15},{3,13... | collective-permute-start | bytes 393224 | tf_op jit(solution)/shard_map/ppermute | solution.py:336
  142.6 12.3 %copy-start.4 = (bf16[1,2,256,128]{3,2,1,0:T(8,128)(2,1)S(1)}, bf16[1,2,256,128]{3,2,1,0:T(8,128)(2,1)}, u32[]{:S(2)}) copy-start(bf16[1,2,256,128]{3,2,1,0:T(8,128)(2,1)} %get-tuple-element.27) | copy-start | bytes 393220
  157.3 5.7 %collective-permute-start.27 = (bf16[1,512,1024]{2,1,0:T(8,128)(2,1)S(1)}, bf16[1,512,1024]{2,1,0:T(8,128)(2,1)S(1)}, u32[]{:S(2)}, u32[]{:S(2)}) collective-permute-start(bf16[1,512,1024]{2,1,0:T(8,128)(2,1)S(1)} %shard_map.70.left_ref.right_ref.own_ref), channel_id=1, source_target_pairs={{0,1},{1,0},{2,3},{3,2},{4,5},{5,4},{6,7},{7,6},{8,9},{9,8},{10,11... | collective-permute-start | bytes 3145736 | tf_op jit(solution)/shard_map/ppermute | solution.py:344
  (14 other events, 77.7 us)
where the time goes:
time: 170 us; the launch traced here: 169 us
  waiting for transfers between devices  57.3 us (34%)
  Pallas kernels  54.9 us (32%)
  starting transfers between devices  48.1 us (28%)
  local copies, waits for them, and re-layouts  6.25 us (4%)
  other arithmetic  1.78 us (1%)
    ppermute x21, waiting for transfers between devices, per_device_fast(): blocks[r] = lax.ppermute(sent, 'stn', partners(stations, r)) if r else sent  56.3 us
    ppermute x21, starting transfers between devices, per_device_fast(): blocks[r] = lax.ppermute(sent, 'stn', partners(stations, r)) if r else sent  38.7 us
    pallas_call x6, Pallas kernels, correlate(): pl.pallas_call(functools.partial(correlate_kernel, rows), grid_spec=pltpu...  29.5 us
    pallas_call x2, Pallas kernels, channelize_dump(): pl.pallas_call(functools.partial(channelize_kernel, len(after)), grid=(st...  13.6 us
    pallas_call x3, Pallas kernels, beams_of(): pl.pallas_call(beam_kernel, grid=(kh,), in_specs=[pl.BlockSpec((1, rows,...  7.56 us
    ppermute x3, starting transfers between devices, per_device_fast(): other = lax.ppermute(own, 'tile', swap)  5.15 us
    pallas_call x4, Pallas kernels, place(): pl.pallas_call(functools.partial(place_kernel, len(blocks)), grid_spec=pl...  4.18 us
    ppermute x3, starting transfers between devices, per_device_fast(): held = [whole, lax.ppermute(whole, 'stn', partners(stations, mask))]  3.48 us
  transfers between devices with their start and end apart: 28, of which 12 were waited for; matrix products, arithmetic and copies ran while one was open for 3% of the time, Pallas kernels for 28%

commit v1 on v0

--- a/solution.py
+++ b/solution.py
@@ -323,23 +323,21 @@
     parts = []
     for dump in range(DUMPS):
         after = [parts[-1][0], stages[0]] if parts else []
-        lead = 1 if dump else kh
-        count = stations * kh // lead
-        parts.append(channelize_dump(turned, table, dump, count, lead, after))
-
-    chunks = [(0, list(range(kh)))] + [(d, [k]) for d in range(1, DUMPS) for k in range(kh)]
+        parts.append(channelize_dump(turned, table, dump, stations * kh, 1, after))
+
+    chunks = [(dump, k) for dump in range(DUMPS) for k in range(kh)]
     arrived = []
-    for dump, ks in chunks:
+    for dump, k in chunks:
         blocks = [None] * stations
         for r in reversed(range(stations)):
-            sent = parts[dump][r if dump == 0 else r * kh + ks[0]][None]
+            sent = parts[dump][r * kh + k][None]
             blocks[r] = lax.ppermute(sent, "stn", partners(stations, r)) if r else sent
         arrived.append(blocks)
 
     visibility, beam_out, weights, after = None, None, None, [stages[1 % len(stages)], parts[-1][0]]
     own_half = tile.reshape(1).astype(jnp.int32)
-    for n, (dump, ks) in enumerate(chunks):
-        first = ks[0] * DUMPS + dump
+    for n, (dump, k) in enumerate(chunks):
+        first = k * DUMPS + dump
         own = place(arrived[n], where, after)
         other = lax.ppermute(own, "tile", swap)
         visibility = correlate(own, own, own_half, slots, first, visibility)
@@ -348,7 +346,7 @@
             spots = me ^ jnp.asarray(order, dtype=jnp.int32)
             weights = place(held, spots, [])
         beam_out = beams_of(weights, own, other, slots, first, beam_out)
-        after = [visibility, beam_out] if n else [visibility]
+        after = [visibility]
     return visibility, beam_out
 
 

time: 170 us -> 195 us (1.15)
  waiting for transfers between devices: 57.3 us -> 81.6 us
  Pallas kernels: 54.9 us -> 58.6 us
    ppermute x21 -> x28, waiting for transfers between devices: 56.3 us -> 72.1 us  [per_device_fast(): blocks[r] = lax.ppermute(sent, 'stn', partners(stations, r)) if r else sent]
    ppermute x3, waiting for transfers between devices: 0.98 us -> 9.43 us  [per_device_fast(): held = [whole, lax.ppermute(whole, 'stn', partners(stations, mask))]]
    pallas_call x6 -> x8, Pallas kernels: 29.5 us -> 32 us  [correlate(): pl.pallas_call(functools.partial(correlate_kernel, rows), grid_spec=pltpu...]
    ppermute x21 -> x28, starting transfers between devices: 38.7 us -> 37.3 us  [per_device_fast(): blocks[r] = lax.ppermute(sent, 'stn', partners(stations, r)) if r else sent]
    ppermute x3 -> x4, starting transfers between devices: 5.15 us -> 4.09 us  [per_device_fast(): other = lax.ppermute(own, 'tile', swap)]
    pallas_call x3 -> x4, Pallas kernels: 7.56 us -> 8.32 us  [beams_of(): pl.pallas_call(beam_kernel, grid=(kh,), in_specs=[pl.BlockSpec((1, rows,...]
    pallas_call x4 -> x5, Pallas kernels: 4.18 us -> 4.7 us  [place(): pl.pallas_call(functools.partial(place_kernel, len(blocks)), grid_spec=pl...]
  transfers between devices with their start and end apart: 28 -> 36, of which waited for: 12 -> 16; matrix products, arithmetic and copies ran while one was open for 3% -> 2% of each run, Pallas kernels for 28% -> 26%
where the time goes in v1:
time: 195 us
  waiting for transfers between devices  81.6 us (42%)
  Pallas kernels  58.6 us (30%)
  starting transfers between devices  46.2 us (24%)
  local copies, waits for them, and re-layouts  5.58 us (3%)
    ppermute x28, waiting for transfers between devices, per_device_fast(): blocks[r] = lax.ppermute(sent, 'stn', partners(stations, r)) if r else sent  72.1 us
    ppermute x28, starting transfers between devices, per_device_fast(): blocks[r] = lax.ppermute(sent, 'stn', partners(stations, r)) if r else sent  37.3 us
    pallas_call x8, Pallas kernels, correlate(): pl.pallas_call(functools.partial(correlate_kernel, rows), grid_spec=pltpu...  32 us
    pallas_call x2, Pallas kernels, channelize_dump(): pl.pallas_call(functools.partial(channelize_kernel, len(after)), grid=(st...  13.6 us
    ppermute x3, waiting for transfers between devices, per_device_fast(): held = [whole, lax.ppermute(whole, 'stn', partners(stations, mask))]  9.43 us
    pallas_call x4, Pallas kernels, beams_of(): pl.pallas_call(beam_kernel, grid=(kh,), in_specs=[pl.BlockSpec((1, rows,...  8.32 us
    pallas_call x5, Pallas kernels, place(): pl.pallas_call(functools.partial(place_kernel, len(blocks)), grid_spec=pl...  4.7 us
    ppermute x4, starting transfers between devices, per_device_fast(): other = lax.ppermute(own, 'tile', swap)  4.09 us
  transfers between devices with their start and end apart: 36, of which 16 were waited for; matrix products, arithmetic and copies ran while one was open for 2% of the time, Pallas kernels for 26%

profile of v1, /device:TPU:9, one launch (start us, length us, event | category | flops | bytes accessed | tf_op | source)
XLA Modules:
  0.0 194.7 jit_solution(9496362101912568301)
XLA Ops:
  4.6 2.4 %collective-permute-start.1 = (bf16[1,2,2,256,128]{4,3,2,1,0:T(8,128)(2,1)S(1)}, bf16[1,2,2,256,128]{4,3,2,1,0:T(8,128)(2,1)S(1)}, u32[]{:S(2)}, u32[]{:S(2)}) collective-permute-start(bf16[1,2,2,256,128]{4,3,2,1,0:T(8,128)(2,1)S(1)} %maximum_bitcast_fusion), channel_id=1, source_target_pairs={{0,8},{2,10},{4,12},{6,14},{8,0},{10,2},{12,4},{14,6},{1,9},{3,11}... | collective-permute-start | bytes 786440 | tf_op jit(solution)/shard_map/ppermute | solution.py:317
  9.1 9.4 %collective-permute-done.1.refs_1_ = bf16[1,2,2,256,128]{4,3,2,1,0:T(8,128)(2,1)S(1)} collective-permute-done((bf16[1,2,2,256,128]{4,3,2,1,0:T(8,128)(2,1)S(1)}, bf16[1,2,2,256,128]{4,3,2,1,0:T(8,128)(2,1)S(1)}, u32[]{:S(2)}, u32[]{:S(2)}) %collective-permute-start.1) | collective-permute-done | bytes 262176 | tf_op jit(solution)/shard_map/ppermute | solution.py:317
  19.5 6.8 %shard_map.59 = (bf16[1,2,256,128]{3,2,1,0:T(8,128)(2,1)}, bf16[1,2,256,128]{3,2,1,0:T(8,128)(2,1)}, bf16[1,2,256,128]{3,2,1,0:T(8,128)(2,1)}, bf16[1,2,256,128]...) custom-call(bf16[256,1056]{1,0:T(8,128)(2,1)} %concatenate.10.table_, ...), custom_call_target="tpu_custom_call" | custom-call | flops 2214592512 | bytes 6291456 | tf_op jit(solution)/shard_map/pallas_call | solution.py:153
  29.1 2.3 %collective-permute-start.26 = (bf16[1,1,2,256,128]{4,3,2,1,0:T(8,128)(2,1)}, bf16[1,1,2,256,128]{4,3,2,1,0:T(8,128)(2,1)S(1)}, u32[]{:S(2)}, u32[]{:S(2)}) collective-permute-start(bf16[1,1,2,256,128]{4,3,2,1,0:T(8,128)(2,1)} %bitcast.92), channel_id=1, source_target_pairs={{0,8},{2,10},{4,12},{6,14},{8,0},{10,2},{12,4},{14,6},{1,9},{3,11}... | collective-permute-start | bytes 393224 | tf_op jit(solution)/shard_map/ppermute | solution.py:334
  31.4 3.1 %collective-permute-start.27 = (bf16[1,1,2,256,128]{4,3,2,1,0:T(8,128)(2,1)}, bf16[1,1,2,256,128]{4,3,2,1,0:T(8,128)(2,1)S(1)}, u32[]{:S(2)}, u32[]{:S(2)}) collective-permute-start(bf16[1,1,2,256,128]{4,3,2,1,0:T(8,128)(2,1)} %bitcast.91), channel_id=1, source_target_pairs={{0,10},{2,8},{4,14},{6,12},{8,2},{10,0},{12,6},{14,4},{1,11},{3,9}... | collective-permute-start | bytes 393224 | tf_op jit(solution)/shard_map/ppermute | solution.py:334
  34.5 2.7 %collective-permute-done.24.refs_2_ = bf16[1,1,2,256,128]{4,3,2,1,0:T(8,128)(2,1)S(1)} collective-permute-done((bf16[1,1,2,256,128]{4,3,2,1,0:T(8,128)(2,1)}, bf16[1,1,2,256,128]{4,3,2,1,0:T(8,128)(2,1)S(1)}, u32[]{:S(2)}, u32[]{:S(2)}) %collective-permute-start.24) | collective-permute-done | bytes 131104 | tf_op jit(solution)/shard_map/ppermute | solution.py:334
  37.2 3.5 %collective-permute-start.28 = (bf16[1,1,2,256,128]{4,3,2,1,0:T(8,128)(2,1)}, bf16[1,1,2,256,128]{4,3,2,1,0:T(8,128)(2,1)S(1)}, u32[]{:S(2)}, u32[]{:S(2)}) collective-permute-start(bf16[1,1,2,256,128]{4,3,2,1,0:T(8,128)(2,1)} %bitcast.90), channel_id=1, source_target_pairs={{0,12},{2,14},{4,8},{6,10},{8,4},{10,6},{12,0},{14,2},{1,13},{3,15... | collective-permute-start | bytes 393224 | tf_op jit(solution)/shard_map/ppermute | solution.py:334
  41.5 3.1 %collective-permute-start.29 = (bf16[1,1,2,256,128]{4,3,2,1,0:T(8,128)(2,1)}, bf16[1,1,2,256,128]{4,3,2,1,0:T(8,128)(2,1)S(1)}, u32[]{:S(2)}, u32[]{:S(2)}) collective-permute-start(bf16[1,1,2,256,128]{4,3,2,1,0:T(8,128)(2,1)} %bitcast.89), channel_id=1, source_target_pairs={{0,14},{2,12},{4,10},{6,8},{8,6},{10,4},{12,2},{14,0},{1,15},{3,13... | collective-permute-start | bytes 393224 | tf_op jit(solution)/shard_map/ppermute | solution.py:334
  44.5 6.8 %shard_map.60 = (bf16[1,2,256,128]{3,2,1,0:T(8,128)(2,1)}, bf16[1,2,256,128]{3,2,1,0:T(8,128)(2,1)}, bf16[1,2,256,128]{3,2,1,0:T(8,128)(2,1)}, bf16[1,2,256,128]...) custom-call(bf16[256,1056]{1,0:T(8,128)(2,1)} %concatenate.10.table_, ...), custom_call_target="tpu_custom_call" | custom-call | flops 2214592512 | bytes 6291456 | tf_op jit(solution)/shard_map/pallas_call | solution.py:153
  51.4 2.7 %collective-permute-done.28.refs_6_ = bf16[1,1,2,256,128]{4,3,2,1,0:T(8,128)(2,1)S(1)} collective-permute-done((bf16[1,1,2,256,128]{4,3,2,1,0:T(8,128)(2,1)}, bf16[1,1,2,256,128]{4,3,2,1,0:T(8,128)(2,1)S(1)}, u32[]{:S(2)}, u32[]{:S(2)}) %collective-permute-start.28) | collective-permute-done | bytes 131104 | tf_op jit(solution)/shard_map/ppermute | solution.py:334
  54.0 3.6 %collective-permute-done.29.refs_7_ = bf16[1,1,2,256,128]{4,3,2,1,0:T(8,128)(2,1)S(1)} collective-permute-done((bf16[1,1,2,256,128]{4,3,2,1,0:T(8,128)(2,1)}, bf16[1,1,2,256,128]{4,3,2,1,0:T(8,128)(2,1)S(1)}, u32[]{:S(2)}, u32[]{:S(2)}) %collective-permute-start.29) | collective-permute-done | bytes 131104 | tf_op jit(solution)/shard_map/ppermute | solution.py:334
  63.5 4.0 %shard_map.62.refs_0_ = bf16[4,2,2048,1024]{3,2,1,0:T(8,128)(2,1)} custom-call(s32[1]{0:T(128)} %bitcast.tile_ref, bf16[1,512,1024]{2,1,0:T(8,128)(2,1)S(1)} %shard_map.61.left_ref.right_ref.own_ref, bf16[1,512,1024]{2,1,0:T(8,128)(2,1)S(1)} %shard_map.61.left_ref.right_ref.own_ref), custom_call_target="tpu_custom_call" | custom-call | flops 2147483648 | bytes 4194304 | tf_op jit(solution)/shard_map/pallas_call | solution.py:236
  67.5 2.4 %collective-permute-start.20 = (bf16[1,1,2,256,128]{4,3,2,1,0:T(8,128)(2,1)S(1)}, bf16[1,1,2,256,128]{4,3,2,1,0:T(8,128)(2,1)S(1)}, u32[]{:S(2)}, u32[]{:S(2)}) collective-permute-start(bf16[1,1,2,256,128]{4,3,2,1,0:T(8,128)(2,1)S(1)} %bitcast.83), channel_id=1, source_target_pairs={{0,10},{2,8},{4,14},{6,12},{8,2},{10,0},{12,6},{14,4},{1,11},{3,9}... | collective-permute-start | bytes 393224 | tf_op jit(solution)/shard_map/ppermute | solution.py:334
  72.3 4.0 %shard_map.63.refs_8_.refs_0_ = bf16[4,2,2048,1024]{3,2,1,0:T(8,128)(2,1)} custom-call(s32[1]{0:T(128)S(6)} %sub.12.tile_ref, bf16[1,512,1024]{2,1,0:T(8,128)(2,1)S(1)} %collective-permute-done.31.left_ref.other_ref, bf16[1,512,1024]{2,1,0:T(8,128)(2,1)S(1)} %shard_map.61.left_ref.right_ref.own_ref, ...), custom_call_target="tpu_custom_call", output_to_operand_aliasing={{}: (3, {})} | custom-call | flops 2147483648 | bytes 4194304 | tf_op jit(solution)/shard_map/pallas_call | solution.py:236
  76.3 6.4 %collective-permute-done.20.refs_5_ = bf16[1,1,2,256,128]{4,3,2,1,0:T(8,128)(2,1)S(1)} collective-permute-done((bf16[1,1,2,256,128]{4,3,2,1,0:T(8,128)(2,1)S(1)}, bf16[1,1,2,256,128]{4,3,2,1,0:T(8,128)(2,1)S(1)}, u32[]{:S(2)}, u32[]{:S(2)}) %collective-permute-start.20) | collective-permute-done | bytes 131104 | tf_op jit(solution)/shard_map/ppermute | solution.py:334
  82.7 3.7 %collective-permute-done.21.refs_6_ = bf16[1,1,2,256,128]{4,3,2,1,0:T(8,128)(2,1)S(1)} collective-permute-done((bf16[1,1,2,256,128]{4,3,2,1,0:T(8,128)(2,1)S(1)}, bf16[1,1,2,256,128]{4,3,2,1,0:T(8,128)(2,1)S(1)}, u32[]{:S(2)}, u32[]{:S(2)}) %collective-permute-start.21) | collective-permute-done | bytes 131104 | tf_op jit(solution)/shard_map/ppermute | solution.py:334
  86.4 3.7 %collective-permute-done.22.refs_7_ = bf16[1,1,2,256,128]{4,3,2,1,0:T(8,128)(2,1)S(1)} collective-permute-done((bf16[1,1,2,256,128]{4,3,2,1,0:T(8,128)(2,1)S(1)}, bf16[1,1,2,256,128]{4,3,2,1,0:T(8,128)(2,1)S(1)}, u32[]{:S(2)}, u32[]{:S(2)}) %collective-permute-start.22) | collective-permute-done | bytes 131104 | tf_op jit(solution)/shard_map/ppermute | solution.py:334
  94.1 2.3 %collective-permute-start.13 = (bf16[1,1,2,256,128]{4,3,2,1,0:T(8,128)(2,1)S(1)}, bf16[1,1,2,256,128]{4,3,2,1,0:T(8,128)(2,1)S(1)}, u32[]{:S(2)}, u32[]{:S(2)}) collective-permute-start(bf16[1,1,2,256,128]{4,3,2,1,0:T(8,128)(2,1)S(1)} %bitcast.78), channel_id=1, source_target_pairs={{0,10},{2,8},{4,14},{6,12},{8,2},{10,0},{12,6},{14,4},{1,11},{3,9}... | collective-permute-start | bytes 393224 | tf_op jit(solution)/shard_map/ppermute | solution.py:334
  96.4 4.0 %shard_map.65.refs_0_ = bf16[4,2,2048,1024]{3,2,1,0:T(8,128)(2,1)} custom-call(s32[1]{0:T(128)} %bitcast.tile_ref, bf16[1,512,1024]{2,1,0:T(8,128)(2,1)S(1)} %shard_map.64.left_ref.right_ref.own_ref, bf16[1,512,1024]{2,1,0:T(8,128)(2,1)S(1)} %shard_map.64.left_ref.right_ref.own_ref, ...), custom_call_target="tpu_custom_call", output_to_operand_aliasing={{}: (3, {})} | custom-call | flops 2147483648 | bytes 4194304 | tf_op jit(solution)/shard_map/pallas_call | solution.py:236
  104.1 4.0 %shard_map.66.refs_8_.refs_0_ = bf16[4,2,2048,1024]{3,2,1,0:T(8,128)(2,1)} custom-call(s32[1]{0:T(128)S(6)} %sub.12.tile_ref, bf16[1,512,1024]{2,1,0:T(8,128)(2,1)S(1)} %collective-permute-done.32.left_ref.other_ref, bf16[1,512,1024]{2,1,0:T(8,128)(2,1)S(1)} %shard_map.64.left_ref.right_ref.own_ref, ...), custom_call_target="tpu_custom_call", output_to_operand_aliasing={{}: (3, {})} | custom-call | flops 2147483648 | bytes 4194304 | tf_op jit(solution)/shard_map/pallas_call | solution.py:236
  108.2 2.4 %collective-permute-done.13.refs_5_ = bf16[1,1,2,256,128]{4,3,2,1,0:T(8,128)(2,1)S(1)} collective-permute-done((bf16[1,1,2,256,128]{4,3,2,1,0:T(8,128)(2,1)S(1)}, bf16[1,1,2,256,128]{4,3,2,1,0:T(8,128)(2,1)S(1)}, u32[]{:S(2)}, u32[]{:S(2)}) %collective-permute-start.13) | collective-permute-done | bytes 131104 | tf_op jit(solution)/shard_map/ppermute | solution.py:334
  110.5 4.3 %collective-permute-done.14.refs_6_ = bf16[1,1,2,256,128]{4,3,2,1,0:T(8,128)(2,1)S(1)} collective-permute-done((bf16[1,1,2,256,128]{4,3,2,1,0:T(8,128)(2,1)S(1)}, bf16[1,1,2,256,128]{4,3,2,1,0:T(8,128)(2,1)S(1)}, u32[]{:S(2)}, u32[]{:S(2)}) %collective-permute-start.14) | collective-permute-done | bytes 131104 | tf_op jit(solution)/shard_map/ppermute | solution.py:334
  114.9 3.1 %collective-permute-done.15.refs_7_ = bf16[1,1,2,256,128]{4,3,2,1,0:T(8,128)(2,1)S(1)} collective-permute-done((bf16[1,1,2,256,128]{4,3,2,1,0:T(8,128)(2,1)S(1)}, bf16[1,1,2,256,128]{4,3,2,1,0:T(8,128)(2,1)S(1)}, u32[]{:S(2)}, u32[]{:S(2)}) %collective-permute-start.15) | collective-permute-done | bytes 131104 | tf_op jit(solution)/shard_map/ppermute | solution.py:334
  123.8 4.0 %shard_map.68.refs_0_ = bf16[4,2,2048,1024]{3,2,1,0:T(8,128)(2,1)} custom-call(s32[1]{0:T(128)} %bitcast.tile_ref, bf16[1,512,1024]{2,1,0:T(8,128)(2,1)S(1)} %shard_map.67.left_ref.right_ref.own_ref, bf16[1,512,1024]{2,1,0:T(8,128)(2,1)S(1)} %shard_map.67.left_ref.right_ref.own_ref, ...), custom_call_target="tpu_custom_call", output_to_operand_aliasing={{}: (3, {})} | custom-call | flops 2147483648 | bytes 4194304 | tf_op jit(solution)/shard_map/pallas_call | solution.py:236
  127.8 22.9 %collective-permute-done.2.refs_1_ = bf16[1,1,2,256,128]{4,3,2,1,0:T(8,128)(2,1)S(1)} collective-permute-done((bf16[1,1,2,256,128]{4,3,2,1,0:T(8,128)(2,1)S(1)}, bf16[1,1,2,256,128]{4,3,2,1,0:T(8,128)(2,1)S(1)}, u32[]{:S(2)}, u32[]{:S(2)}) %collective-permute-start.2) | collective-permute-done | bytes 131104 | tf_op jit(solution)/shard_map/ppermute | solution.py:334
  150.8 2.7 %collective-permute-start.6 = (bf16[1,1,2,256,128]{4,3,2,1,0:T(8,128)(2,1)S(1)}, bf16[1,1,2,256,128]{4,3,2,1,0:T(8,128)(2,1)S(1)}, u32[]{:S(2)}, u32[]{:S(2)}) collective-permute-start(bf16[1,1,2,256,128]{4,3,2,1,0:T(8,128)(2,1)S(1)} %bitcast.70), channel_id=1, source_target_pairs={{0,10},{2,8},{4,14},{6,12},{8,2},{10,0},{12,6},{14,4},{1,11},{3,9}... | collective-permute-start | bytes 393224 | tf_op jit(solution)/shard_map/ppermute | solution.py:334
  155.6 4.0 %shard_map.69.refs_8_.refs_0_ = bf16[4,2,2048,1024]{3,2,1,0:T(8,128)(2,1)} custom-call(s32[1]{0:T(128)S(6)} %sub.12.tile_ref, bf16[1,512,1024]{2,1,0:T(8,128)(2,1)S(1)} %collective-permute-done.33.left_ref.other_ref, bf16[1,512,1024]{2,1,0:T(8,128)(2,1)S(1)} %shard_map.67.left_ref.right_ref.own_ref, ...), custom_call_target="tpu_custom_call", output_to_operand_aliasing={{}: (3, {})} | custom-call | flops 2147483648 | bytes 4194304 | tf_op jit(solution)/shard_map/pallas_call | solution.py:236
  159.6 7.9 %collective-permute-done.6.refs_5_ = bf16[1,1,2,256,128]{4,3,2,1,0:T(8,128)(2,1)S(1)} collective-permute-done((bf16[1,1,2,256,128]{4,3,2,1,0:T(8,128)(2,1)S(1)}, bf16[1,1,2,256,128]{4,3,2,1,0:T(8,128)(2,1)S(1)}, u32[]{:S(2)}, u32[]{:S(2)}) %collective-permute-start.6) | collective-permute-done | bytes 131104 | tf_op jit(solution)/shard_map/ppermute | solution.py:334
  167.4 4.3 %collective-permute-done.7.refs_6_ = bf16[1,1,2,256,128]{4,3,2,1,0:T(8,128)(2,1)S(1)} collective-permute-done((bf16[1,1,2,256,128]{4,3,2,1,0:T(8,128)(2,1)S(1)}, bf16[1,1,2,256,128]{4,3,2,1,0:T(8,128)(2,1)S(1)}, u32[]{:S(2)}, u32[]{:S(2)}) %collective-permute-start.7) | collective-permute-done | bytes 131104 | tf_op jit(solution)/shard_map/ppermute | solution.py:334
  171.7 2.9 %collective-permute-done.8.refs_7_ = bf16[1,1,2,256,128]{4,3,2,1,0:T(8,128)(2,1)S(1)} collective-permute-done((bf16[1,1,2,256,128]{4,3,2,1,0:T(8,128)(2,1)S(1)}, bf16[1,1,2,256,128]{4,3,2,1,0:T(8,128)(2,1)S(1)}, u32[]{:S(2)}, u32[]{:S(2)}) %collective-permute-start.8) | collective-permute-done | bytes 131104 | tf_op jit(solution)/shard_map/ppermute | solution.py:334
  184.6 4.0 %shard_map.71.refs_0_ = bf16[4,2,2048,1024]{3,2,1,0:T(8,128)(2,1)} custom-call(s32[1]{0:T(128)} %bitcast.tile_ref, bf16[1,512,1024]{2,1,0:T(8,128)(2,1)S(1)} %shard_map.70.left_ref.right_ref.own_ref, bf16[1,512,1024]{2,1,0:T(8,128)(2,1)S(1)} %shard_map.70.left_ref.right_ref.own_ref, ...), custom_call_target="tpu_custom_call", output_to_operand_aliasing={{}: (3, {})} | custom-call | flops 2147483648 | bytes 4194304 | tf_op jit(solution)/shard_map/pallas_call | solution.py:236
  190.7 4.0 %shard_map.72 = bf16[4,2,2048,1024]{3,2,1,0:T(8,128)(2,1)} custom-call(s32[1]{0:T(128)S(6)} %sub.12.tile_ref, bf16[1,512,1024]{2,1,0:T(8,128)(2,1)S(1)} %collective-permute-done.34.left_ref.other_ref, bf16[1,512,1024]{2,1,0:T(8,128)(2,1)S(1)} %shard_map.70.left_ref.right_ref.own_ref, ...), custom_call_target="tpu_custom_call", output_to_operand_aliasing={{}: (3, {})} | custom-call | flops 2147483648 | bytes 4194304 | tf_op jit(solution)/shard_map/pallas_call | solution.py:236
  (135 shorter events, 46.3 us)
Async XLA Ops:
  4.6 14.0 %collective-permute-start.1 = (bf16[1,2,2,256,128]{4,3,2,1,0:T(8,128)(2,1)S(1)}, bf16[1,2,2,256,128]{4,3,2,1,0:T(8,128)(2,1)S(1)}, u32[]{:S(2)}, u32[]{:S(2)}) collective-permute-start(bf16[1,2,2,256,128]{4,3,2,1,0:T(8,128)(2,1)S(1)} %maximum_bitcast_fusion), channel_id=1, source_target_pairs={{0,8},{2,10},{4,12},{6,14},{8,0},{10,2},{12,4},{14,6},{1,9},{3,11}... | collective-permute-start | bytes 786440 | tf_op jit(solution)/shard_map/ppermute | solution.py:317
  18.6 39.0 %collective-permute-start.30 = (bf16[2,2,2,256,128]{4,3,2,1,0:T(8,128)(2,1)S(1)}, bf16[2,2,2,256,128]{4,3,2,1,0:T(8,128)(2,1)S(1)}, u32[]{:S(2)}, u32[]{:S(2)}) collective-permute-start(bf16[2,2,2,256,128]{4,3,2,1,0:T(8,128)(2,1)S(1)} %pad_maximum_fusion.1), channel_id=1, source_target_pairs={{0,4},{2,6},{4,0},{6,2},{8,12},{10,14},{12,8},{14,10},{1,5},{3,7},... | collective-permute-start | bytes 1572872 | tf_op jit(solution)/shard_map/ppermute | solution.py:317
  27.4 9.8 %collective-permute-start.24 = (bf16[1,1,2,256,128]{4,3,2,1,0:T(8,128)(2,1)}, bf16[1,1,2,256,128]{4,3,2,1,0:T(8,128)(2,1)S(1)}, u32[]{:S(2)}, u32[]{:S(2)}) collective-permute-start(bf16[1,1,2,256,128]{4,3,2,1,0:T(8,128)(2,1)} %bitcast.94), channel_id=1, source_target_pairs={{0,4},{2,6},{4,0},{6,2},{8,12},{10,14},{12,8},{14,10},{1,5},{3,7},... | collective-permute-start | bytes 393224 | tf_op jit(solution)/shard_map/ppermute | solution.py:334
  28.3 13.2 %collective-permute-start.25 = (bf16[1,1,2,256,128]{4,3,2,1,0:T(8,128)(2,1)}, bf16[1,1,2,256,128]{4,3,2,1,0:T(8,128)(2,1)S(1)}, u32[]{:S(2)}, u32[]{:S(2)}) collective-permute-start(bf16[1,1,2,256,128]{4,3,2,1,0:T(8,128)(2,1)} %bitcast.93), channel_id=1, source_target_pairs={{0,6},{2,4},{4,2},{6,0},{8,14},{10,12},{12,10},{14,8},{1,7},{3,5},... | collective-permute-start | bytes 393224 | tf_op jit(solution)/shard_map/ppermute | solution.py:334
  29.1 22.3 %collective-permute-start.26 = (bf16[1,1,2,256,128]{4,3,2,1,0:T(8,128)(2,1)}, bf16[1,1,2,256,128]{4,3,2,1,0:T(8,128)(2,1)S(1)}, u32[]{:S(2)}, u32[]{:S(2)}) collective-permute-start(bf16[1,1,2,256,128]{4,3,2,1,0:T(8,128)(2,1)} %bitcast.92), channel_id=1, source_target_pairs={{0,8},{2,10},{4,12},{6,14},{8,0},{10,2},{12,4},{14,6},{1,9},{3,11}... | collective-permute-start | bytes 393224 | tf_op jit(solution)/shard_map/ppermute | solution.py:334
  31.4 20.0 %collective-permute-start.27 = (bf16[1,1,2,256,128]{4,3,2,1,0:T(8,128)(2,1)}, bf16[1,1,2,256,128]{4,3,2,1,0:T(8,128)(2,1)S(1)}, u32[]{:S(2)}, u32[]{:S(2)}) collective-permute-start(bf16[1,1,2,256,128]{4,3,2,1,0:T(8,128)(2,1)} %bitcast.91), channel_id=1, source_target_pairs={{0,10},{2,8},{4,14},{6,12},{8,2},{10,0},{12,6},{14,4},{1,11},{3,9}... | collective-permute-start | bytes 393224 | tf_op jit(solution)/shard_map/ppermute | solution.py:334
  37.2 16.8 %collective-permute-start.28 = (bf16[1,1,2,256,128]{4,3,2,1,0:T(8,128)(2,1)}, bf16[1,1,2,256,128]{4,3,2,1,0:T(8,128)(2,1)S(1)}, u32[]{:S(2)}, u32[]{:S(2)}) collective-permute-start(bf16[1,1,2,256,128]{4,3,2,1,0:T(8,128)(2,1)} %bitcast.90), channel_id=1, source_target_pairs={{0,12},{2,14},{4,8},{6,10},{8,4},{10,6},{12,0},{14,2},{1,13},{3,15... | collective-permute-start | bytes 393224 | tf_op jit(solution)/shard_map/ppermute | solution.py:334
  41.5 16.1 %collective-permute-start.29 = (bf16[1,1,2,256,128]{4,3,2,1,0:T(8,128)(2,1)}, bf16[1,1,2,256,128]{4,3,2,1,0:T(8,128)(2,1)S(1)}, u32[]{:S(2)}, u32[]{:S(2)}) collective-permute-start(bf16[1,1,2,256,128]{4,3,2,1,0:T(8,128)(2,1)} %bitcast.89), channel_id=1, source_target_pairs={{0,14},{2,12},{4,10},{6,8},{8,6},{10,4},{12,2},{14,0},{1,15},{3,13... | collective-permute-start | bytes 393224 | tf_op jit(solution)/shard_map/ppermute | solution.py:334
  60.3 9.9 %collective-permute-start.31 = (bf16[1,512,1024]{2,1,0:T(8,128)(2,1)S(1)}, bf16[1,512,1024]{2,1,0:T(8,128)(2,1)S(1)}, u32[]{:S(2)}, u32[]{:S(2)}) collective-permute-start(bf16[1,512,1024]{2,1,0:T(8,128)(2,1)S(1)} %shard_map.61.left_ref.right_ref.own_ref), channel_id=1, source_target_pairs={{0,1},{1,0},{2,3},{3,2},{4,5},{5,4},{6,7},{7,6},{8,9},{9,8},{10,11... | collective-permute-start | bytes 3145736 | tf_op jit(solution)/shard_map/ppermute | solution.py:342
  61.2 15.1 %collective-permute-start.18 = (bf16[1,1,2,256,128]{4,3,2,1,0:T(8,128)(2,1)}, bf16[1,1,2,256,128]{4,3,2,1,0:T(8,128)(2,1)S(1)}, u32[]{:S(2)}, u32[]{:S(2)}) collective-permute-start(bf16[1,1,2,256,128]{4,3,2,1,0:T(8,128)(2,1)} %bitcast.86), channel_id=1, source_target_pairs={{0,6},{2,4},{4,2},{6,0},{8,14},{10,12},{12,10},{14,8},{1,7},{3,5},... | collective-permute-start | bytes 393224 | tf_op jit(solution)/shard_map/ppermute | solution.py:334
  63.5 12.8 %collective-permute-start.19 = (bf16[1,1,2,256,128]{4,3,2,1,0:T(8,128)(2,1)}, bf16[1,1,2,256,128]{4,3,2,1,0:T(8,128)(2,1)S(1)}, u32[]{:S(2)}, u32[]{:S(2)}) collective-permute-start(bf16[1,1,2,256,128]{4,3,2,1,0:T(8,128)(2,1)} %bitcast.85), channel_id=1, source_target_pairs={{0,8},{2,10},{4,12},{6,14},{8,0},{10,2},{12,4},{14,6},{1,9},{3,11}... | collective-permute-start | bytes 393224 | tf_op jit(solution)/shard_map/ppermute | solution.py:334
  67.5 15.2 %collective-permute-start.20 = (bf16[1,1,2,256,128]{4,3,2,1,0:T(8,128)(2,1)S(1)}, bf16[1,1,2,256,128]{4,3,2,1,0:T(8,128)(2,1)S(1)}, u32[]{:S(2)}, u32[]{:S(2)}) collective-permute-start(bf16[1,1,2,256,128]{4,3,2,1,0:T(8,128)(2,1)S(1)} %bitcast.83), channel_id=1, source_target_pairs={{0,10},{2,8},{4,14},{6,12},{8,2},{10,0},{12,6},{14,4},{1,11},{3,9}... | collective-permute-start | bytes 393224 | tf_op jit(solution)/shard_map/ppermute | solution.py:334
  70.0 16.4 %collective-permute-start.21 = (bf16[1,1,2,256,128]{4,3,2,1,0:T(8,128)(2,1)S(1)}, bf16[1,1,2,256,128]{4,3,2,1,0:T(8,128)(2,1)S(1)}, u32[]{:S(2)}, u32[]{:S(2)}) collective-permute-start(bf16[1,1,2,256,128]{4,3,2,1,0:T(8,128)(2,1)S(1)} %bitcast.82), channel_id=1, source_target_pairs={{0,12},{2,14},{4,8},{6,10},{8,4},{10,6},{12,0},{14,2},{1,13},{3,15... | collective-permute-start | bytes 393224 | tf_op jit(solution)/shard_map/ppermute | solution.py:334
  70.1 20.0 %collective-permute-start.22 = (bf16[1,1,2,256,128]{4,3,2,1,0:T(8,128)(2,1)S(1)}, bf16[1,1,2,256,128]{4,3,2,1,0:T(8,128)(2,1)S(1)}, u32[]{:S(2)}, u32[]{:S(2)}) collective-permute-start(bf16[1,1,2,256,128]{4,3,2,1,0:T(8,128)(2,1)S(1)} %bitcast.80), channel_id=1, source_target_pairs={{0,14},{2,12},{4,10},{6,8},{8,6},{10,4},{12,2},{14,0},{1,15},{3,13... | collective-permute-start | bytes 393224 | tf_op jit(solution)/shard_map/ppermute | solution.py:334
  91.0 11.3 %collective-permute-start.32 = (bf16[1,512,1024]{2,1,0:T(8,128)(2,1)S(1)}, bf16[1,512,1024]{2,1,0:T(8,128)(2,1)S(1)}, u32[]{:S(2)}, u32[]{:S(2)}) collective-permute-start(bf16[1,512,1024]{2,1,0:T(8,128)(2,1)S(1)} %shard_map.64.left_ref.right_ref.own_ref), channel_id=1, source_target_pairs={{0,1},{1,0},{2,3},{3,2},{4,5},{5,4},{6,7},{7,6},{8,9},{9,8},{10,11... | collective-permute-start | bytes 3145736 | tf_op jit(solution)/shard_map/ppermute | solution.py:342
  91.6 8.8 %collective-permute-start.10 = (bf16[1,1,2,256,128]{4,3,2,1,0:T(8,128)(2,1)S(1)}, bf16[1,1,2,256,128]{4,3,2,1,0:T(8,128)(2,1)S(1)}, u32[]{:S(2)}, u32[]{:S(2)}) collective-permute-start(bf16[1,1,2,256,128]{4,3,2,1,0:T(8,128)(2,1)S(1)} %bitcast.84), channel_id=1, source_target_pairs={{0,4},{2,6},{4,0},{6,2},{8,12},{10,14},{12,8},{14,10},{1,5},{3,7},... | collective-permute-start | bytes 393224 | tf_op jit(solution)/shard_map/ppermute | solution.py:334
  91.6 10.8 %collective-permute-start.11 = (bf16[1,1,2,256,128]{4,3,2,1,0:T(8,128)(2,1)S(1)}, bf16[1,1,2,256,128]{4,3,2,1,0:T(8,128)(2,1)S(1)}, u32[]{:S(2)}, u32[]{:S(2)}) collective-permute-start(bf16[1,1,2,256,128]{4,3,2,1,0:T(8,128)(2,1)S(1)} %bitcast.81), channel_id=1, source_target_pairs={{0,6},{2,4},{4,2},{6,0},{8,14},{10,12},{12,10},{14,8},{1,7},{3,5},... | collective-permute-start | bytes 393224 | tf_op jit(solution)/shard_map/ppermute | solution.py:334
  93.0 15.2 %collective-permute-start.12 = (bf16[1,1,2,256,128]{4,3,2,1,0:T(8,128)(2,1)S(1)}, bf16[1,1,2,256,128]{4,3,2,1,0:T(8,128)(2,1)S(1)}, u32[]{:S(2)}, u32[]{:S(2)}) collective-permute-start(bf16[1,1,2,256,128]{4,3,2,1,0:T(8,128)(2,1)S(1)} %bitcast.79), channel_id=1, source_target_pairs={{0,8},{2,10},{4,12},{6,14},{8,0},{10,2},{12,4},{14,6},{1,9},{3,11}... | collective-permute-start | bytes 393224 | tf_op jit(solution)/shard_map/ppermute | solution.py:334
  94.1 16.4 %collective-permute-start.13 = (bf16[1,1,2,256,128]{4,3,2,1,0:T(8,128)(2,1)S(1)}, bf16[1,1,2,256,128]{4,3,2,1,0:T(8,128)(2,1)S(1)}, u32[]{:S(2)}, u32[]{:S(2)}) collective-permute-start(bf16[1,1,2,256,128]{4,3,2,1,0:T(8,128)(2,1)S(1)} %bitcast.78), channel_id=1, source_target_pairs={{0,10},{2,8},{4,14},{6,12},{8,2},{10,0},{12,6},{14,4},{1,11},{3,9}... | collective-permute-start | bytes 393224 | tf_op jit(solution)/shard_map/ppermute | solution.py:334
  100.4 14.5 %collective-permute-start.14 = (bf16[1,1,2,256,128]{4,3,2,1,0:T(8,128)(2,1)S(1)}, bf16[1,1,2,256,128]{4,3,2,1,0:T(8,128)(2,1)S(1)}, u32[]{:S(2)}, u32[]{:S(2)}) collective-permute-start(bf16[1,1,2,256,128]{4,3,2,1,0:T(8,128)(2,1)S(1)} %bitcast.77), channel_id=1, source_target_pairs={{0,12},{2,14},{4,8},{6,10},{8,4},{10,6},{12,0},{14,2},{1,13},{3,15... | collective-permute-start | bytes 393224 | tf_op jit(solution)/shard_map/ppermute | solution.py:334
  102.3 15.6 %collective-permute-start.15 = (bf16[1,1,2,256,128]{4,3,2,1,0:T(8,128)(2,1)S(1)}, bf16[1,1,2,256,128]{4,3,2,1,0:T(8,128)(2,1)S(1)}, u32[]{:S(2)}, u32[]{:S(2)}) collective-permute-start(bf16[1,1,2,256,128]{4,3,2,1,0:T(8,128)(2,1)S(1)} %bitcast.76), channel_id=1, source_target_pairs={{0,14},{2,12},{4,10},{6,8},{8,6},{10,4},{12,2},{14,0},{1,15},{3,13... | collective-permute-start | bytes 393224 | tf_op jit(solution)/shard_map/ppermute | solution.py:334
  102.4 15.6 %collective-permute-start.9 = (bf16[1,1,2,256,128]{4,3,2,1,0:T(8,128)(2,1)S(1)}, bf16[1,1,2,256,128]{4,3,2,1,0:T(8,128)(2,1)S(1)}, u32[]{:S(2)}, u32[]{:S(2)}) collective-permute-start(bf16[1,1,2,256,128]{4,3,2,1,0:T(8,128)(2,1)S(1)} %bitcast.75), channel_id=1, source_target_pairs={{0,2},{2,0},{4,6},{6,4},{8,10},{10,8},{12,14},{14,12},{1,3},{3,1},... | collective-permute-start | bytes 393224 | tf_op jit(solution)/shard_map/ppermute | solution.py:334
  118.8 35.6 %collective-permute-start.33 = (bf16[1,512,1024]{2,1,0:T(8,128)(2,1)S(1)}, bf16[1,512,1024]{2,1,0:T(8,128)(2,1)S(1)}, u32[]{:S(2)}, u32[]{:S(2)}) collective-permute-start(bf16[1,512,1024]{2,1,0:T(8,128)(2,1)S(1)} %shard_map.67.left_ref.right_ref.own_ref), channel_id=1, source_target_pairs={{0,1},{1,0},{2,3},{3,2},{4,5},{5,4},{6,7},{7,6},{8,9},{9,8},{10,11... | collective-permute-start | bytes 3145736 | tf_op jit(solution)/shard_map/ppermute | solution.py:342
  120.4 56.7 %collective-permute-start.35 = (bf16[4,2,2,256,128]{4,3,2,1,0:T(8,128)(2,1)S(1)}, bf16[4,2,2,256,128]{4,3,2,1,0:T(8,128)(2,1)S(1)}, u32[]{:S(2)}, u32[]{:S(2)}) collective-permute-start(bf16[4,2,2,256,128]{4,3,2,1,0:T(8,128)(2,1)S(1)} %pad_maximum_fusion.refs_0_), channel_id=1, source_target_pairs={{0,2},{2,0},{4,6},{6,4},{8,10},{10,8},{12,14},{14,12},{1,3},{3,1},... | collective-permute-start | bytes 3145736 | tf_op jit(solution)/shard_map/ppermute | solution.py:317
  121.1 29.7 %collective-permute-start.2 = (bf16[1,1,2,256,128]{4,3,2,1,0:T(8,128)(2,1)S(1)}, bf16[1,1,2,256,128]{4,3,2,1,0:T(8,128)(2,1)S(1)}, u32[]{:S(2)}, u32[]{:S(2)}) collective-permute-start(bf16[1,1,2,256,128]{4,3,2,1,0:T(8,128)(2,1)S(1)} %bitcast.74), channel_id=1, source_target_pairs={{0,2},{2,0},{4,6},{6,4},{8,10},{10,8},{12,14},{14,12},{1,3},{3,1},... | collective-permute-start | bytes 393224 | tf_op jit(solution)/shard_map/ppermute | solution.py:334
  121.9 28.8 %collective-permute-start.3 = (bf16[1,1,2,256,128]{4,3,2,1,0:T(8,128)(2,1)S(1)}, bf16[1,1,2,256,128]{4,3,2,1,0:T(8,128)(2,1)S(1)}, u32[]{:S(2)}, u32[]{:S(2)}) collective-permute-start(bf16[1,1,2,256,128]{4,3,2,1,0:T(8,128)(2,1)S(1)} %bitcast.73), channel_id=1, source_target_pairs={{0,4},{2,6},{4,0},{6,2},{8,12},{10,14},{12,8},{14,10},{1,5},{3,7},... | collective-permute-start | bytes 393224 | tf_op jit(solution)/shard_map/ppermute | solution.py:334
  122.0 31.5 %collective-permute-start.4 = (bf16[1,1,2,256,128]{4,3,2,1,0:T(8,128)(2,1)S(1)}, bf16[1,1,2,256,128]{4,3,2,1,0:T(8,128)(2,1)S(1)}, u32[]{:S(2)}, u32[]{:S(2)}) collective-permute-start(bf16[1,1,2,256,128]{4,3,2,1,0:T(8,128)(2,1)S(1)} %bitcast.72), channel_id=1, source_target_pairs={{0,6},{2,4},{4,2},{6,0},{8,14},{10,12},{12,10},{14,8},{1,7},{3,5},... | collective-permute-start | bytes 393224 | tf_op jit(solution)/shard_map/ppermute | solution.py:334
  150.8 8.8 %collective-permute-start.5 = (bf16[1,1,2,256,128]{4,3,2,1,0:T(8,128)(2,1)S(1)}, bf16[1,1,2,256,128]{4,3,2,1,0:T(8,128)(2,1)S(1)}, u32[]{:S(2)}, u32[]{:S(2)}) collective-permute-start(bf16[1,1,2,256,128]{4,3,2,1,0:T(8,128)(2,1)S(1)} %bitcast.71), channel_id=1, source_target_pairs={{0,8},{2,10},{4,12},{6,14},{8,0},{10,2},{12,4},{14,6},{1,9},{3,11}... | collective-permute-start | bytes 393224 | tf_op jit(solution)/shard_map/ppermute | solution.py:334
  150.8 16.7 %collective-permute-start.6 = (bf16[1,1,2,256,128]{4,3,2,1,0:T(8,128)(2,1)S(1)}, bf16[1,1,2,256,128]{4,3,2,1,0:T(8,128)(2,1)S(1)}, u32[]{:S(2)}, u32[]{:S(2)}) collective-permute-start(bf16[1,1,2,256,128]{4,3,2,1,0:T(8,128)(2,1)S(1)} %bitcast.70), channel_id=1, source_target_pairs={{0,10},{2,8},{4,14},{6,12},{8,2},{10,0},{12,6},{14,4},{1,11},{3,9}... | collective-permute-start | bytes 393224 | tf_op jit(solution)/shard_map/ppermute | solution.py:334
  153.5 18.2 %collective-permute-start.7 = (bf16[1,1,2,256,128]{4,3,2,1,0:T(8,128)(2,1)S(1)}, bf16[1,1,2,256,128]{4,3,2,1,0:T(8,128)(2,1)S(1)}, u32[]{:S(2)}, u32[]{:S(2)}) collective-permute-start(bf16[1,1,2,256,128]{4,3,2,1,0:T(8,128)(2,1)S(1)} %bitcast.69), channel_id=1, source_target_pairs={{0,12},{2,14},{4,8},{6,10},{8,4},{10,6},{12,0},{14,2},{1,13},{3,15... | collective-permute-start | bytes 393224 | tf_op jit(solution)/shard_map/ppermute | solution.py:334
  154.4 20.3 %collective-permute-start.8 = (bf16[1,1,2,256,128]{4,3,2,1,0:T(8,128)(2,1)S(1)}, bf16[1,1,2,256,128]{4,3,2,1,0:T(8,128)(2,1)S(1)}, u32[]{:S(2)}, u32[]{:S(2)}) collective-permute-start(bf16[1,1,2,256,128]{4,3,2,1,0:T(8,128)(2,1)S(1)} %bitcast.68), channel_id=1, source_target_pairs={{0,14},{2,12},{4,10},{6,8},{8,6},{10,4},{12,2},{14,0},{1,15},{3,13... | collective-permute-start | bytes 393224 | tf_op jit(solution)/shard_map/ppermute | solution.py:334
  175.5 13.1 %collective-permute-start.34 = (bf16[1,512,1024]{2,1,0:T(8,128)(2,1)S(1)}, bf16[1,512,1024]{2,1,0:T(8,128)(2,1)S(1)}, u32[]{:S(2)}, u32[]{:S(2)}) collective-permute-start(bf16[1,512,1024]{2,1,0:T(8,128)(2,1)S(1)} %shard_map.70.left_ref.right_ref.own_ref), channel_id=1, source_target_pairs={{0,1},{1,0},{2,3},{3,2},{4,5},{5,4},{6,7},{7,6},{8,9},{9,8},{10,11... | collective-permute-start | bytes 3145736 | tf_op jit(solution)/shard_map/ppermute | solution.py:342
  (29 other events, 515.3 us)
